TPU v7x, 256 devices: a whole 4x4x8 slice. The times are simulated.
256 devices in a mesh: member: 16 (over y, x), section: 8 (over z), tensor: 2 (over core).
Axes of the slice: x: 4, y: 4, z: 8, core: 2. Of those that a mesh axis runs over, the one named last changes fastest.
Arguments:
- hidden_input: bfloat16 [16, 8, 2, 128, 4096], P('member', 'section'), may hold values from -6 to 6
- document_index: int32 [8, 2, 128], P('section'), may hold values from 0 to 7, never falling along the last dimension, each value on 1 to 32 neighbouring positions
- query_key_value_weight: bfloat16 [8, 4096, 4, 768], P('section', 'member', 'tensor'), may hold values from -0.09375 to 0.09375
- output_weight: bfloat16 [8, 2048, 4096], P('section', 'tensor', 'member'), may hold values from -0.125 to 0.125
- adapter_down: bfloat16 [16, 8, 2048, 16], P('member', 'section', 'tensor'), may hold values from -0.125 to 0.125
- adapter_up: bfloat16 [16, 8, 16, 4096], P('member', 'section'), may hold values from -1.5 to 1.5
- attention_gain: float32 [16, 8, 4096], P('member', 'section'), may hold values from 0.6 to 5, as said below
- final_norm_gain: float32 [16, 4096], P('member', 'tensor'), may hold values from 0.25 to 1.75
Outputs:
- averaged: bfloat16 [8, 2, 128, 4096], P('section', None, None, 'tensor')
Inputs may be any that keep to these rules, and one draw needn't show every extreme that they name: `document_index`: along each micro-batch the document number never falls; each document spans at most 32 positions and one spans exactly that many. `attention_gain`: positive gains.
All inputs are finite; a program needn't handle non-finite values.
Results may differ from a plain program's by a relative error of at most 0.038.
The roundings to bfloat16 on the way count: a program that leaves them out, or rounds other values in their place, can miss the bound.
Values may be sent and summed in bfloat16 or wider, within the bound.
A program may use at most 128 MiB of HBM per device.

v0:
```python
import math

import jax
import jax.numpy as jnp
from jax import lax
from jax.sharding import PartitionSpec as P

HEAD_WIDTH = 128
TICKS = 2


def shifted(block, axis, distance):
    devices = range(lax.axis_size(axis))
    route = [((i - distance) % len(devices), i) for i in devices]
    return lax.ppermute(block, axis, route)


def norm_rows(values, gain_row):
    return values * lax.rsqrt(jnp.mean(values * values, axis=-1, keepdims=True) + 1e-05) * gain_row


def rope_tables(seq_len, head_dim):
    position = jnp.arange(seq_len, dtype=jnp.float32)
    frequency = jnp.exp(
        jnp.arange(head_dim // 2, dtype=jnp.float32) * (-2.0 * math.log(500000.0) / head_dim)
    )
    angles = position[:, None] * frequency[None, :]
    return (jnp.cos(angles), jnp.sin(angles))


def rotate(values, cosine_table, sine_table):
    half_dim = values.shape[-1] // 2
    first_half = values[..., :half_dim]
    second_half = values[..., half_dim:]
    bcast_shape = (1, values.shape[1]) + (1,) * (values.ndim - 3) + (half_dim,)
    cosine_part = cosine_table.reshape(bcast_shape)
    sine_part = sine_table.reshape(bcast_shape)
    return jnp.concatenate(
        [
            first_half * cosine_part - second_half * sine_part,
            second_half * cosine_part + first_half * sine_part,
        ],
        axis=-1,
    )


def attention(projected, doc_rows):
    group_size = projected.shape[3] - 2
    seq_len = projected.shape[1]
    head_dim = projected.shape[-1]
    cosine_table, sine_table = rope_tables(seq_len, head_dim)
    queries = rotate(projected[:, :, :, :group_size, :], cosine_table, sine_table).astype(
        jnp.bfloat16
    )
    key_rows = rotate(projected[:, :, :, group_size, :], cosine_table, sine_table).astype(
        jnp.bfloat16
    )
    value_rows = projected[:, :, :, group_size + 1, :].astype(jnp.bfloat16)
    scores = jnp.einsum(
        "bskgd,btkd->bkgst", queries, key_rows, preferred_element_type=jnp.float32
    ) / math.sqrt(head_dim)
    position = jnp.arange(seq_len)
    causal = position[:, None] >= position[None, :]
    same_doc = doc_rows[:, :, None] == doc_rows[:, None, :]
    allowed = (causal[None] & same_doc)[:, None, None]
    scores = jnp.where(allowed, scores, -1e30)
    row_max = jnp.max(scores, axis=-1, keepdims=True)
    weights = jnp.exp(scores - row_max)
    weights = (weights / jnp.sum(weights, axis=-1, keepdims=True)).astype(jnp.bfloat16)
    context = jnp.einsum(
        "bkgst,btkd->bskgd", weights, value_rows, preferred_element_type=jnp.float32
    )
    return context.astype(jnp.bfloat16).reshape(doc_rows.shape[0] * seq_len, -1)


def per_device(
    hidden_input,
    document_index,
    query_key_value_weight,
    output_weight,
    adapter_down,
    adapter_up,
    attention_gain,
    final_norm_gain,
):
    hidden = hidden_input[0, 0]
    doc_rows = document_index[0]
    batch_count, seq_len, model_dim = hidden.shape
    token_count = batch_count * seq_len
    local_heads = query_key_value_weight.shape[2]
    qkv_full, out_full = (
        lax.all_gather(query_key_value_weight, "member", axis=1, tiled=True),
        lax.all_gather(output_weight, "member", axis=2, tiled=True),
    )
    qkv_matrix = qkv_full[0].reshape(model_dim, -1)
    gain_row = attention_gain[0, 0]
    down_matrix = adapter_down[0, 0]
    up_matrix = adapter_up[0, 0]
    for tick_step in range(TICKS):
        hidden_f = hidden.astype(jnp.float32)
        normed = norm_rows(hidden_f, gain_row).astype(jnp.bfloat16).reshape(token_count, model_dim)
        projected = jnp.dot(normed, qkv_matrix, preferred_element_type=jnp.float32)
        projected = projected.reshape(batch_count, seq_len, local_heads, -1, HEAD_WIDTH)
        context = attention(projected, doc_rows)
        main_term = jnp.dot(context, out_full[0], preferred_element_type=jnp.float32)
        low_rank = jnp.dot(context, down_matrix, preferred_element_type=jnp.float32).astype(
            jnp.bfloat16
        )
        partial_value = (
            (main_term + jnp.dot(low_rank, up_matrix, preferred_element_type=jnp.float32))
            .astype(jnp.bfloat16)
            .astype(jnp.float32)
        )
        summed = lax.psum(partial_value.astype(jnp.bfloat16), "tensor").astype(jnp.float32)
        updated = (hidden_f.reshape(token_count, model_dim) + summed).astype(jnp.bfloat16)
        updated, doc_rows = shifted((updated, doc_rows), "section", 1)
        hidden = updated.reshape(batch_count, seq_len, model_dim)
    hidden_f = hidden.astype(jnp.float32)
    inverse = lax.rsqrt(jnp.mean(hidden_f * hidden_f, axis=-1, keepdims=True) + 1e-05)
    feature_count = final_norm_gain.shape[1]
    columns = lax.dynamic_slice_in_dim(
        hidden_f, lax.axis_index("tensor") * feature_count, feature_count, 2
    )
    normed_rows = columns * inverse * final_norm_gain[0]
    summed = lax.psum(normed_rows.astype(jnp.bfloat16), "member").astype(jnp.float32)
    return (summed / lax.axis_size("member")).astype(jnp.bfloat16)[None]


def solution(mesh):
    return jax.shard_map(
        per_device,
        mesh=mesh,
        in_specs=(
            P("member", "section", None, None, None),
            P("section", None, None),
            P("section", "member", "tensor", None),
            P("section", "tensor", "member"),
            P("member", "section", "tensor", None),
            P("member", "section", None, None),
            P("member", "section", None),
            P("member", "tensor"),
        ),
        out_specs=P("section", None, None, "tensor"),
        check_vma=False,
    )
```

profile of v0, /device:TPU:1, one launch (start us, length us, event | category | flops | bytes accessed | tf_op | source)
XLA Modules:
  0.0 510.0 jit_solution(3478900847534683961)
XLA Ops:
  6.5 0.7 all-gather.3.cloned.1.call-update
  7.3 0.7 all-gather.5.cloned.1.call-update
  8.1 2.5 collective-permute-start.1
  10.6 2.1 multiply_reduce_fusion.1
  12.9 2.8 collective-permute-done.1
  15.9 92.8 %all-gather.3.cloned.1.call-done = bf16[1,4096,2,768]{3,2,0,1:T(2,128)(2,1)} async-done(((bf16[1,256,2,768]{3,2,0,1:T(2,128)(2,1)}), bf16[1,4096,2,768]{3,2,0,1:T(2,128)(2,1)}) %all-gather.3.cloned.1.call-update) | async-done | bytes 12582928 | tf_op jit(solution)/shard_map/all_gather | solution.py:92
  108.6 31.2 %copy.48 = bf16[1,4096,2,768]{1,3,2,0:T(8,128)(2,1)} copy(bf16[1,4096,2,768]{3,2,0,1:T(2,128)(2,1)} %all-gather.3.cloned.1.call-done) | data formatting | bytes 25165824 | tf_op jit(solution)/shard_map/reshape;squeeze | solution.py:95
  139.8 7.2 %fusion.14 = f32[2,128,2,6,128]{1,4,3,2,0:T(8,128)S(1)} fusion(bf16[2,6,128,4096,1]{3,2,1,0,4:T(8,128)(2,1)} %bitcast.139, bf16[1,1,2,128,4096]{4,3,2,1,0:T(8,128)(2,1)S(1)} %copy-done.1, f32[4096]{0:T(1024)S(1)} %bitcast.144, f32[2,128]{1,0:T(2,128)S(1)} %add_rsqrt_fusion.1), kind=kOutput, calls=%fused_computation.23 | convolution fusion | flops 3225419776 | bytes 16270336 | tf_op jit(solution)/shard_map/dot_general | solution.py:102
  147.1 1.1 copy-done.3
  148.3 1.1 fusion.103
  149.5 1.6 fusion.26
  151.8 41.5 %all-gather.5.cloned.1.call-done = bf16[1,1024,4096]{2,1,0:T(8,128)(2,1)} async-done(((bf16[1,1024,256]{2,1,0:T(8,128)(2,1)}), bf16[1,1024,4096]{2,1,0:T(8,128)(2,1)}) %all-gather.5.cloned.1.call-update) | async-done | bytes 8388624 | tf_op jit(solution)/shard_map/all_gather | solution.py:93
  193.3 7.7 %fusion.4 = f32[256,4096]{1,0:T(8,128)} fusion(bf16[256,1024]{1,0:T(8,128)(2,1)S(1)} %reshape.207, bf16[1,1024,4096]{2,1,0:T(8,128)(2,1)} %all-gather.5.cloned.1.call-done), kind=kOutput, calls=%fused_computation.4 | convolution fusion | flops 2147483648 | bytes 13107200 | tf_op jit(solution)/shard_map/dot_general | solution.py:105
  201.0 4.8 fusion.6
  205.9 33.1 %all-reduce.4.cloned.1.call-done = bf16[256,4096]{1,0:T(8,128)(2,1)} async-done(((bf16[256,4096]{1,0:T(8,128)(2,1)}), bf16[256,4096]{1,0:T(8,128)(2,1)}) %all-reduce.4.cloned.1.call-update) | async-done | bytes 2097168 | tf_op jit(solution)/shard_map/psum | solution.py:114
  239.0 2.4 fusion.12
  241.4 1.3 collective-permute-start
  242.6 47.4 %collective-permute-done = bf16[256,4096]{1,0:T(8,128)(2,1)S(1)} collective-permute-done((bf16[256,4096]{1,0:T(8,128)(2,1)S(1)}, bf16[256,4096]{1,0:T(8,128)(2,1)S(1)}, u32[]{:S(2)}, u32[]{:S(2)}) %collective-permute-start) | collective-permute-done | bytes 2097184 | tf_op jit(solution)/shard_map/ppermute | solution.py:15
  290.6 0.6 fusion.10
  291.2 7.3 %fusion.109 = f32[2,128,2,6,128]{1,4,3,2,0:T(8,128)S(1)} fusion(bf16[2,128,4096,1,1]{2,1,4,3,0:T(8,128)(2,1)S(1)} %bitcast.142, bf16[2,6,128,4096,1]{3,2,1,0,4:T(8,128)(2,1)} %bitcast.140), kind=kOutput, calls=%fused_computation.110 | convolution fusion | flops 3221225472 | bytes 16252928 | tf_op jit(solution)/shard_map/dot_general | solution.py:102
  298.6 1.1 copy-done.2
  299.9 0.5 fusion.106
  300.5 1.6 fusion.27
  302.8 7.6 %fusion.2 = f32[256,4096]{1,0:T(8,128)} fusion(bf16[256,1024]{1,0:T(8,128)(2,1)S(1)} %reshape.208, bf16[1,1024,4096]{2,1,0:T(8,128)(2,1)} %all-gather.5.cloned.1.call-done), kind=kOutput, calls=%fused_computation.2 | convolution fusion | flops 2147483648 | bytes 13107200 | tf_op jit(solution)/shard_map/dot_general | solution.py:105
  310.5 4.8 fusion.7
  315.3 34.0 %all-reduce.6.cloned.1.call-done = bf16[256,4096]{1,0:T(8,128)(2,1)} async-done(((bf16[256,4096]{1,0:T(8,128)(2,1)}), bf16[256,4096]{1,0:T(8,128)(2,1)}) %all-reduce.6.cloned.1.call-update) | async-done | bytes 2097168 | tf_op jit(solution)/shard_map/psum | solution.py:114
  349.3 3.7 fusion.11
  353.0 1.0 collective-permute-start.2
  354.0 47.6 %collective-permute-done.2 = bf16[256,4096]{1,0:T(8,128)(2,1)S(1)} collective-permute-done((bf16[256,4096]{1,0:T(8,128)(2,1)}, bf16[256,4096]{1,0:T(8,128)(2,1)S(1)}, u32[]{:S(2)}, u32[]{:S(2)}) %collective-permute-start.2) | collective-permute-done | bytes 2097184 | tf_op jit(solution)/shard_map/ppermute | solution.py:15
  402.8 1.2 multiply_convert_fusion.2
  404.0 97.0 %all-reduce.8.cloned.1.call-done = bf16[2,128,2048]{2,1,0:T(8,128)(2,1)} async-done(((bf16[2,128,2048]{2,1,0:T(8,128)(2,1)}), bf16[2,128,2048]{2,1,0:T(8,128)(2,1)}) %all-reduce.8.cloned.1.call-update) | async-done | bytes 1048592 | tf_op jit(solution)/shard_map/psum | solution.py:125
  501.1 2.4 fusion.28
  (42 shorter events, 4.0 us)
Async XLA Ops:
  6.5 194.5 %copy-start = (bf16[1,1,16,4096]{3,2,1,0:T(8,128)(2,1)S(1)}, bf16[1,1,16,4096]{3,2,1,0:T(8,128)(2,1)}, u32[]{:S(2)}) copy-start(bf16[1,1,16,4096]{3,2,1,0:T(8,128)(2,1)} %param.13) | copy-start | bytes 393220
  6.5 9.2 %copy-start.7 = (s32[1,2,128]{2,1,0:T(2,128)S(1)}, s32[1,2,128]{2,1,0:T(2,128)}, u32[]{:S(2)}) copy-start(s32[1,2,128]{2,1,0:T(2,128)} %param.9) | copy-start | bytes 3076
  6.5 102.1 %all-gather.3.cloned.1.call-start = ((), (), s32[]{:S(2)}) async-start(), calls=%async_computation | async-start | bytes 13369344 | tf_op jit(solution)/shard_map/all_gather | solution.py:92
  7.3 186.1 %all-gather.5.cloned.1.call-start = ((), (), s32[]{:S(2)}) async-start(), calls=%async_computation.1 | async-start | bytes 8912896 | tf_op jit(solution)/shard_map/all_gather | solution.py:93
  8.0 231.0 %all-reduce.4.cloned.1.call-start = ((), (), s32[]{:S(2)}) async-start(), calls=%async_computation.2 | async-start | bytes 4194304 | tf_op jit(solution)/shard_map/psum | solution.py:114
  8.1 7.7 %collective-permute-start.1 = (s32[2,128]{1,0:T(2,128)}, s32[2,128]{1,0:T(2,128)S(1)}, u32[]{:S(2)}, u32[]{:S(2)}) collective-permute-start(s32[2,128]{1,0:T(2,128)} %bitcast.147), channel_id=1, source_target_pairs={{14,0},{0,2},{2,4},{4,6},{6,8},{8,10},{10,12},{12,14},{15,1},{1,3}... | collective-permute-start | bytes 3080 | tf_op jit(solution)/shard_map/ppermute | solution.py:15
  15.9 124.0 %copy-start.1 = (bf16[1,1,2,128,4096]{4,3,2,1,0:T(8,128)(2,1)S(1)}, bf16[1,1,2,128,4096]{4,3,2,1,0:T(8,128)(2,1)}, u32[]{:S(2)}) copy-start(bf16[1,1,2,128,4096]{4,3,2,1,0:T(8,128)(2,1)} %param.8) | copy-start | bytes 6291460
  15.9 124.0 %copy-start.5 = (f32[1,1,4096]{2,1,0:T(1,128)S(1)}, f32[1,1,4096]{2,1,0:T(1,128)}, u32[]{:S(2)}) copy-start(f32[1,1,4096]{2,1,0:T(1,128)} %param.14) | copy-start | bytes 49156
  147.0 1.2 copy-start.3
  151.8 49.2 %copy-start.4 = (bf16[1,1,1024,16]{2,3,1,0:T(8,128)(2,1)S(1)}, bf16[1,1,1024,16]{2,3,1,0:T(8,128)(2,1)}, u32[]{:S(2)}) copy-start(bf16[1,1,1024,16]{2,3,1,0:T(8,128)(2,1)} %param.12) | copy-start | bytes 98308
  205.8 143.5 %all-reduce.6.cloned.1.call-start = ((), (), s32[]{:S(2)}) async-start(), calls=%async_computation.3 | async-start | bytes 4194304 | tf_op jit(solution)/shard_map/psum | solution.py:114
  241.4 48.7 %collective-permute-start = (bf16[256,4096]{1,0:T(8,128)(2,1)S(1)}, bf16[256,4096]{1,0:T(8,128)(2,1)S(1)}, u32[]{:S(2)}, u32[]{:S(2)}) collective-permute-start(bf16[256,4096]{1,0:T(8,128)(2,1)S(1)} %fusion.12), channel_id=1, source_target_pairs={{14,0},{0,2},{2,4},{4,6},{6,8},{8,10},{10,12},{12,14},{15,1},{1,3}... | collective-permute-start | bytes 6291464 | tf_op jit(solution)/shard_map/ppermute | solution.py:15
  298.6 1.2 copy-start.2
  315.2 185.8 %all-reduce.8.cloned.1.call-start = ((), (), s32[]{:S(2)}) async-start(), calls=%async_computation.4 | async-start | bytes 2097152 | tf_op jit(solution)/shard_map/psum | solution.py:125
  353.0 48.6 %collective-permute-start.2 = (bf16[256,4096]{1,0:T(8,128)(2,1)}, bf16[256,4096]{1,0:T(8,128)(2,1)S(1)}, u32[]{:S(2)}, u32[]{:S(2)}) collective-permute-start(bf16[256,4096]{1,0:T(8,128)(2,1)} %fusion.11), channel_id=1, source_target_pairs={{14,0},{0,2},{2,4},{4,6},{6,8},{8,10},{10,12},{12,14},{15,1},{1,3}... | collective-permute-start | bytes 6291464 | tf_op jit(solution)/shard_map/ppermute | solution.py:15
  402.1 0.7 copy-start.6
Sparse Core Ops, SparseCore 0:
  9.8 98.8 all-gather.2
  111.0 82.2 all-gather.4
  205.9 33.0 all-reduce.3
  315.4 33.8 all-reduce.5
  404.2 96.8 all-reduce.7
where the time goes:
time: 512 us; the launch traced here: 510 us
  waiting for transfers between devices  398 us (78%)
  matrix products  44.3 us (9%)
  local copies, waits for them, and re-layouts  35 us (7%)
  other arithmetic  14.6 us (3%)
  between operations  13.3 us (3%)
    ppermute x3, waiting for transfers between devices, shifted(): return lax.ppermute(block, axis, route)  97.8 us
    psum x1, waiting for transfers between devices, per_device(): lax.psum(normed_rows.astype(jnp.bfloat16), 'member').astype(jnp.float32)  97 us
    all_gather x1, waiting for transfers between devices, per_device(): lax.all_gather(query_key_value_weight, 'member', axis=1, tiled=True)  92.8 us
    psum x2, waiting for transfers between devices, per_device(): lax.psum(partial_value.astype(jnp.bfloat16), 'tensor').astype(jnp.float32)  67.2 us
    all_gather x1, waiting for transfers between devices, per_device(): lax.all_gather(output_weight, 'member', axis=2, tiled=True)  41.5 us
    another operation x1, local copies, waits for them, and re-layouts, per_device(): qkv_matrix = qkv_full[0].reshape(model_dim, -1)  31.2 us
    dot_general x2, matrix products, per_device(): jnp.dot(context, out_full[0], preferred_element_type=jnp.float32)  15.3 us
    dot_general x2, matrix products, per_device(): projected = jnp.dot(normed, qkv_matrix, preferred_element_type=jnp.float32)  14.5 us
  transfers between devices with their start and end apart: 8, of which 8 were waited for; matrix products, arithmetic and copies ran while one was open for 9% of the time, Pallas kernels for 0%

commit v1 on v0

v1 whole, which is shorter than its diff:
```python
import math

import jax
import jax.numpy as jnp
import numpy as np
from jax import lax
from jax.experimental import pallas as pl
from jax.experimental.pallas import tpu as pltpu
from jax.sharding import PartitionSpec as P

HEAD_WIDTH = 128
GROUP = 4
WIDTH = 4096
ROWS = 256
SEQ = 128
MEMBERS = 16
SIDE = 4
EPS = 1e-05
MESH = pl.DeviceIdType.MESH
F32 = jnp.float32
BF16 = jnp.bfloat16


def rope_tables():
    position = np.arange(SEQ, dtype=np.float32)
    frequency = np.exp(
        np.arange(HEAD_WIDTH // 2, dtype=np.float32)
        * np.float32(-2.0 * math.log(500000.0) / HEAD_WIDTH)
    ).astype(np.float32)
    angles = (position[:, None] * frequency[None, :]).astype(np.float32)
    cosine, sine = np.cos(angles), np.sin(angles)
    return (
        np.concatenate([cosine, cosine], axis=1).astype(np.float32),
        np.concatenate([-sine, sine], axis=1).astype(np.float32),
    )


def wrap(value):
    return lax.rem(value + 2 * SIDE, SIDE)


class Torus:
    def __init__(self):
        self.member = lax.axis_index("member")
        self.x = lax.rem(self.member, SIDE)
        self.y = self.member // SIDE

    def at(self, part, du, dv):
        dx, dy = (du, dv) if part == 0 else (dv, du)
        return wrap(self.y + dy) * SIDE + wrap(self.x + dx)


class Gather:
    order = (0, -1, 1, 2)

    def __init__(self, torus, own, slot, whole, send_sem, recv_sem):
        self.torus, self.own, self.slot, self.whole = torus, own, slot, whole
        self.send_sem, self.recv_sem = send_sem, recv_sem

    def start(self, src, dst, part, du, dv, index):
        pltpu.make_async_remote_copy(
            src_ref=src,
            dst_ref=dst,
            send_sem=self.send_sem.at[part],
            recv_sem=self.recv_sem.at[part, index],
            device_id={"member": self.torus.at(part, du, dv)},
            device_id_type=MESH,
        ).start()

    def wait(self, part, du, dv, index):
        ref = self.slot(part, self.torus.at(part, du, dv), None)
        pltpu.make_async_remote_copy(
            src_ref=ref,
            dst_ref=ref,
            send_sem=self.send_sem.at[part],
            recv_sem=self.recv_sem.at[part, index],
            device_id={"member": self.torus.at(part, 1, 0)},
            device_id_type=MESH,
        ).wait_recv()

    def full(self, part, du, dv):
        return self.slot(part, self.torus.at(part, du, dv), None)

    def half(self, part, du, dv, which):
        return self.slot(part, self.torus.at(part, du, dv), which)

    def spread(self, part, q):
        du = self.order[q]
        here = self.full(part, du, 0)
        src = self.own(part) if q == 0 else here
        self.start(src, here, part, 0, 1, 3 + q)
        self.start(src, here, part, 0, -1, 7 + q)

    def first(self, part):
        here = self.full(part, 0, 0)
        self.start(self.own(part), here, part, 1, 0, 0)
        self.start(self.own(part), here, part, -1, 0, 1)

    def line(self, part):
        self.wait(part, -1, 0, 0)
        ref = self.half(part, -1, 0, 0)
        self.start(ref, ref, part, 1, 0, 2)
        self.spread(part, 1)
        self.wait(part, 1, 0, 1)
        ref = self.half(part, 1, 0, 1)
        self.start(ref, ref, part, -1, 0, 2)
        self.spread(part, 2)

    def far(self, part):
        self.wait(part, 2, 0, 2)
        self.spread(part, 3)

    def cross(self, part, q):
        du = self.order[q]
        self.wait(part, du, -1, 3 + q)
        ref = self.half(part, du, -1, 0)
        self.start(ref, ref, part, 0, 1, 11 + q)
        self.wait(part, du, 1, 7 + q)
        ref = self.half(part, du, 1, 1)
        self.start(ref, ref, part, 0, -1, 11 + q)

    def last(self, part, q):
        self.wait(part, self.order[q], 2, 11 + q)

    def sent(self, part):
        ref = self.whole(part)
        pltpu.make_async_remote_copy(
            src_ref=ref,
            dst_ref=ref,
            send_sem=self.send_sem.at[part],
            recv_sem=self.recv_sem.at[part, 0],
            device_id={"member": self.torus.at(part, 1, 0)},
            device_id_type=MESH,
        ).wait_send()


def rotate(values, cosine, sine):
    return (values * cosine + pltpu.roll(values, HEAD_WIDTH // 2, 1) * sine).astype(BF16)


def kernel(
    hidden_in, docs_in, qkv_in, out_in, down_ref, up_ref, gain_ref, final_ref, cos_ref, sin_ref,
    out_ref,
    wq, wo, hv, nrm, proj, ctx, low, docs_next,
    own_part, peer_send, peer_recv, h_send, h_next,
    part2, send2, recv2, h_last, square, square_peer, rows_out, rows_in, mean_own, mean_in,
    ag_send, ag_recv, local_sem, peer_s, peer_r, hop_s, hop_r, fwd_s, fwd_r,
    two_s, two_r, misc_s, misc_r, scatter_s, scatter_r,
):
    torus = Torus()
    member = torus.member
    section = lax.axis_index("section")
    tensor = lax.axis_index("tensor")
    other = 1 - tensor
    sections = 8
    after = lax.rem(section + 1, sections)
    before = lax.rem(section + sections - 1, sections)

    barrier = pltpu.get_barrier_semaphore()

    def greet(i, carry):
        pl.semaphore_signal(
            barrier, inc=1, device_id={"member": lax.rem(member + i, MEMBERS)}, device_id_type=MESH
        )
        return carry

    lax.fori_loop(1, MEMBERS, greet, 0)
    pl.semaphore_signal(barrier, inc=1, device_id={"tensor": other}, device_id_type=MESH)
    pl.semaphore_signal(barrier, inc=1, device_id={"section": after}, device_id_type=MESH)
    pl.semaphore_signal(barrier, inc=1, device_id={"section": before}, device_id_type=MESH)

    load_h = pltpu.make_async_copy(hidden_in, hv, local_sem.at[0])
    load_h.start()
    pl.semaphore_wait(barrier, MEMBERS + 2)

    def qkv_slot(part, slot, which):
        lower = pl.multiple_of(slot * 256 + part * 128 + (64 if which == 1 else 0), 64)
        return wq.at[pl.ds(lower, 128 if which is None else 64)]

    qkv = Gather(
        torus,
        lambda part: qkv_in.at[pl.ds(part * 128, 128)],
        qkv_slot,
        lambda part: wq.at[pl.ds(0, 15 * 128)],
        ag_send.at[0],
        ag_recv.at[0],
    )

    def out_slot(part, slot, which):
        if which is None:
            return wo.at[slot, part]
        return wo.at[slot, part, pl.ds(which * 512, 512)]

    outw = Gather(
        torus,
        lambda part: out_in.at[:, pl.ds(part * 128, 128)],
        out_slot,
        lambda part: wo.at[pl.ds(0, 15), part],
        ag_send.at[1],
        ag_recv.at[1],
    )
    both = (0, 1)
    for part in both:
        qkv.first(part)
    for part in both:
        qkv.spread(part, 0)

    own_rows = pl.ds(pl.multiple_of(member * 256, 256), 256)
    load_q = pltpu.make_async_copy(qkv_in, wq.at[own_rows], local_sem.at[1])
    load_q.start()
    load_o = [
        pltpu.make_async_copy(
            out_in.at[:, pl.ds(part * 128, 128)], wo.at[member, part], local_sem.at[2 + part]
        )
        for part in both
    ]
    for copy in load_o:
        copy.start()
    pass_docs = pltpu.make_async_remote_copy(
        docs_in, docs_next, misc_s.at[0], misc_r.at[0], {"section": after}, MESH
    )
    pass_docs.start()
    load_h.wait()

    def norm_first(i, carry):
        rows = pl.ds(pl.multiple_of(i * 16, 16), 16)
        h = hv[rows, :].astype(F32)
        scale = lax.rsqrt(jnp.mean(h * h, axis=-1, keepdims=True) + EPS)
        nrm[rows, :] = (h * scale * gain_ref[...]).astype(BF16)
        return carry

    lax.fori_loop(0, ROWS // 16, norm_first, 0)

    def project():
        def block(n, carry):
            columns = pl.ds(pl.multiple_of(n * 256, 256), 256)
            proj[:, columns] = jnp.dot(nrm[...], wq[:, columns], preferred_element_type=F32)
            return carry

        lax.fori_loop(0, 6, block, 0)

    ahead = lax.broadcasted_iota(jnp.int32, (SEQ, SEQ), 0) >= lax.broadcasted_iota(
        jnp.int32, (SEQ, SEQ), 1
    )

    def attend(docs_ref):
        for batch in range(2):
            numbers = jnp.broadcast_to(docs_ref[batch : batch + 1, :], (SEQ, SEQ)).astype(F32)
            allowed = ahead & (numbers == numbers.T)
            allowed = jnp.concatenate([allowed.astype(F32)] * GROUP, axis=0) > 0.5
            rows = slice(batch * SEQ, (batch + 1) * SEQ)
            cosine, sine = cos_ref[...], sin_ref[...]

            def head(k, carry):
                base = k * (GROUP + 2) * HEAD_WIDTH

                def piece(g):
                    return proj[rows, pl.ds(pl.multiple_of(base + g * 128, 128), 128)]

                queries = jnp.concatenate(
                    [rotate(piece(g), cosine, sine) for g in range(GROUP)], axis=0
                )
                keys = rotate(piece(GROUP), cosine, sine)
                values = piece(GROUP + 1).astype(BF16)
                scores = lax.dot_general(
                    queries, keys, (((1,), (1,)), ((), ())), preferred_element_type=F32
                ) * (1.0 / math.sqrt(HEAD_WIDTH))
                scores = jnp.where(allowed, scores, -1e30)
                weights = jnp.exp(scores - jnp.max(scores, axis=-1, keepdims=True))
                weights = (weights / jnp.sum(weights, axis=-1, keepdims=True)).astype(BF16)
                context = jnp.dot(weights, values, preferred_element_type=F32).astype(BF16)
                for g in range(GROUP):
                    columns = pl.ds(pl.multiple_of(k * 512 + g * 128, 128), 128)
                    ctx[rows, columns] = context[g * SEQ : (g + 1) * SEQ]
                return carry

            lax.fori_loop(0, 2, head, 0)
        low[...] = lax.dot_general(
            ctx[...], down_ref[...], (((1,), (1,)), ((), ())), preferred_element_type=F32
        ).astype(BF16)

    for part in both:
        qkv.line(part)
    for part in both:
        qkv.cross(part, 0)
    for part in both:
        qkv.far(part)
    for q in (1, 2, 3):
        for part in both:
            qkv.cross(part, q)
    for part in both:
        outw.first(part)
    for part in both:
        outw.spread(part, 0)
    for q in range(SIDE):
        for part in both:
            qkv.last(part, q)
    load_q.wait()
    project()
    for part in both:
        outw.line(part)
    attend(docs_in)
    for copy in load_o:
        copy.wait()

    def slot_of(part, du, dv):
        dx = jnp.where(part == 0, du, dv)
        dy = jnp.where(part == 0, dv, du)
        return wrap(torus.y + dy) * SIDE + wrap(torus.x + dx)

    def column_of(part, slot):
        return pl.ds(pl.multiple_of(slot * 256 + part * 128, 128), 128)

    def partial(part, slot):
        main = jnp.dot(ctx[...], wo[slot, part], preferred_element_type=F32)
        return (
            main + jnp.dot(low[...], up_ref[:, column_of(part, slot)], preferred_element_type=F32)
        ).astype(BF16)

    def peer_copy(i):
        return pltpu.make_async_remote_copy(
            peer_send.at[i], peer_recv.at[i], peer_s.at[i], peer_r.at[i], {"tensor": other}, MESH
        )

    def hop_copy(i, slot):
        return pltpu.make_async_remote_copy(
            h_send.at[i], h_next.at[tensor, slot], hop_s.at[i], hop_r.at[i], {"section": after}, MESH
        )

    def forward_copy(i, part, slot):
        ref = h_next.at[part, slot]
        return pltpu.make_async_remote_copy(
            ref, ref, fwd_s.at[i], fwd_r.at[i], {"tensor": other}, MESH
        )

    def start_block(i, du, dv):
        peer_send[i] = partial(other, slot_of(other, du, dv))
        peer_copy(i).start()
        own_part[i] = partial(tensor, slot_of(tensor, du, dv))

    def finish_block(i, du, dv):
        slot = slot_of(tensor, du, dv)
        peer_copy(i).wait_recv()
        total = own_part[i].astype(F32) + peer_recv[i].astype(F32)
        h_send[i] = (hv[:, column_of(tensor, slot)].astype(F32) + total).astype(BF16)
        hop_copy(i, slot).start()

    def arrive(i, du, dv):
        slot = slot_of(tensor, du, dv)
        hop_copy(i, slot).wait_recv()
        forward_copy(i, tensor, slot).start()

    order = Gather.order
    blocks = [(q, 0) for q in range(4)]
    for q in range(4):
        blocks += [(q, -1), (q, 1)]
    blocks += [(q, 2) for q in range(4)]
    progress = [0, 0]

    def run(count):
        for i in range(count[0], count[1]):
            q, dv = blocks[i]
            start_block(i, order[q], dv)
            if i >= 1:
                q, dv = blocks[i - 1]
                finish_block(i - 1, order[q], dv)
            if i >= 4:
                q, dv = blocks[i - 4]
                arrive(i - 4, order[q], dv)

    run((0, 1))
    for part in both:
        outw.cross(part, 0)
    run((1, 3))
    for part in both:
        outw.far(part)
    run((3, 4))
    for q in (1, 2, 3):
        for part in both:
            outw.cross(part, q)
        run((4 + 2 * (q - 1), 6 + 2 * (q - 1)))
    run((10, 12))
    for q in range(SIDE):
        for part in both:
            outw.last(part, q)
        run((12 + q, 13 + q))
    q, dv = blocks[15]
    finish_block(15, order[q], dv)
    for i in range(12, 16):
        q, dv = blocks[i]
        arrive(i, order[q], dv)
    for i in range(16):
        q, dv = blocks[i]
        forward_copy(i, other, slot_of(other, order[q], dv)).wait_recv()
    pass_docs.wait_recv()

    def norm_second(i, carry):
        rows = pl.ds(pl.multiple_of(i * 32, 32), 32)
        total = jnp.zeros((32, 128), F32)
        for slot in range(MEMBERS):
            for part in both:
                h = h_next[part, slot, rows, :].astype(F32)
                total = total + h * h
        scale = lax.rsqrt(jnp.sum(total, axis=-1, keepdims=True) * (1.0 / WIDTH) + EPS)
        scale = jnp.broadcast_to(scale, (32, 128))
        for slot in range(MEMBERS):
            for part in both:
                columns = slice(slot * 256 + part * 128, slot * 256 + part * 128 + 128)
                h = h_next[part, slot, rows, :].astype(F32)
                nrm[rows, columns] = (h * scale * gain_ref[:, columns]).astype(BF16)
        return carry

    lax.fori_loop(0, ROWS // 32, norm_second, 0)
    project()
    attend(docs_next)

    def partial_pair(slot):
        weights = jnp.concatenate([wo[slot, 0], wo[slot, 1]], axis=1)
        columns = pl.ds(pl.multiple_of(slot * 256, 256), 256)
        main = jnp.dot(ctx[...], weights, preferred_element_type=F32)
        return (main + jnp.dot(low[...], up_ref[:, columns], preferred_element_type=F32)).astype(BF16)

    def two_copy(i):
        return pltpu.make_async_remote_copy(
            send2.at[i], recv2.at[i], two_s.at[i], two_r.at[i], {"tensor": other}, MESH
        )

    def give(i, carry):
        send2[i] = partial_pair(other * 8 + i)
        two_copy(i).start()
        return carry

    lax.fori_loop(0, 8, give, 0)

    def keep(i, carry):
        part2[i] = partial_pair(tensor * 8 + i)
        return carry

    lax.fori_loop(0, 8, keep, 0)
    square[...] = jnp.zeros_like(square)

    def settle(i, carry):
        two_copy(i).wait_recv()
        slot = tensor * 8 + i
        for part in both:
            cols = slice(part * 128, part * 128 + 128)
            total = part2[i, :, cols].astype(F32) + recv2[i, :, cols].astype(F32)
            h = (h_next[part, slot].astype(F32) + total).astype(BF16)
            h_last[i, :, cols] = h
            h = h.astype(F32)
            square[...] += h * h
        return carry

    lax.fori_loop(0, 8, settle, 0)
    swap = pltpu.make_async_remote_copy(
        square, square_peer, misc_s.at[1], misc_r.at[1], {"tensor": other}, MESH
    )
    swap.start()
    swap.wait()

    def norm_last(i, carry):
        rows = pl.ds(pl.multiple_of(i * 32, 32), 32)
        total = square[rows, :] + square_peer[rows, :]
        scale = lax.rsqrt(jnp.sum(total, axis=-1, keepdims=True) * (1.0 / WIDTH) + EPS)
        scale = jnp.broadcast_to(scale, (32, 256))
        for j in range(8):
            columns = slice(j * 256, j * 256 + 256)
            h = h_last[j, rows, :].astype(F32)
            rows_out[rows, columns] = (h * scale * final_ref[:, columns]).astype(BF16)
        return carry

    lax.fori_loop(0, ROWS // 32, norm_last, 0)

    def scatter_copy(i):
        target = lax.rem(member + i, MEMBERS)
        return pltpu.make_async_remote_copy(
            rows_out.at[pl.ds(pl.multiple_of(target * 16, 16), 16)],
            rows_in.at[member],
            scatter_s,
            scatter_r,
            {"member": target},
            MESH,
        )

    def scatter(i, carry):
        scatter_copy(i).start()
        return carry

    lax.fori_loop(1, MEMBERS, scatter, 0)
    pltpu.make_async_copy(
        rows_out.at[pl.ds(pl.multiple_of(member * 16, 16), 16)], rows_in.at[member], local_sem.at[4]
    ).start()
    pltpu.make_async_copy(
        rows_out.at[pl.ds(pl.multiple_of(member * 16, 16), 16)], rows_in.at[member], local_sem.at[4]
    ).wait()
    fifteen = pltpu.make_async_remote_copy(
        rows_in.at[pl.ds(0, 15)], rows_in.at[pl.ds(0, 15)], scatter_s, scatter_r,
        {"tensor": other}, MESH,
    )
    fifteen.wait_recv()
    total = rows_in[0].astype(F32)
    for m in range(1, MEMBERS):
        total = total + rows_in[m].astype(F32)
    mean_own[...] = (total * (1.0 / MEMBERS)).astype(BF16)
    hop = pltpu.make_async_remote_copy(
        mean_own, mean_in, misc_s.at[2], misc_r.at[2], {"section": after}, MESH
    )
    hop.start()
    hop.wait_recv()

    def mean_slot(part, slot, which):
        rows = pl.ds(pl.multiple_of(slot * 16, 16), 16)
        lower = part * 1024 + (512 if which == 1 else 0)
        return out_ref.at[rows, pl.ds(lower, 1024 if which is None else 512)]

    final = Gather(
        torus,
        lambda part: mean_in.at[:, pl.ds(part * 1024, 1024)],
        mean_slot,
        lambda part: out_ref.at[pl.ds(0, 240), pl.ds(0, 1024)],
        ag_send.at[2],
        ag_recv.at[2],
    )
    for part in both:
        final.first(part)
    for part in both:
        final.spread(part, 0)
    out_ref[pl.ds(pl.multiple_of(member * 16, 16), 16), :] = mean_in[...]
    for part in both:
        final.line(part)
    for part in both:
        final.cross(part, 0)
    for part in both:
        final.far(part)
    for q in (1, 2, 3):
        for part in both:
            final.cross(part, q)
    for q in range(SIDE):
        for part in both:
            final.last(part, q)

    for gather in (qkv, outw, final):
        for part in both:
            gather.sent(part)
    for i in range(16):
        q, dv = blocks[i]
        peer_copy(i).wait_send()
        slot = slot_of(tensor, order[q], dv)
        hop_copy(i, slot).wait_send()
        forward_copy(i, tensor, slot).wait_send()
    for i in range(8):
        two_copy(i).wait_send()
    pass_docs.wait_send()
    hop.wait_send()
    fifteen.wait_send()


def per_device(
    hidden_input,
    document_index,
    query_key_value_weight,
    output_weight,
    adapter_down,
    adapter_up,
    attention_gain,
    final_norm_gain,
):
    cosine, sine = rope_tables()
    vmem = pl.BlockSpec(memory_space=pltpu.VMEM)
    anywhere = pl.BlockSpec(memory_space=pl.ANY)
    dma = pltpu.SemaphoreType.DMA
    averaged = pl.pallas_call(
        kernel,
        out_shape=jax.ShapeDtypeStruct((ROWS, WIDTH // 2), BF16),
        in_specs=[anywhere, vmem, anywhere, anywhere] + [vmem] * 6,
        out_specs=vmem,
        scratch_shapes=[
            pltpu.VMEM((WIDTH, 1536), BF16),
            pltpu.VMEM((MEMBERS, 2, 1024, 128), BF16),
            pltpu.VMEM((ROWS, WIDTH), BF16),
            pltpu.VMEM((ROWS, WIDTH), BF16),
            pltpu.VMEM((ROWS, 1536), F32),
            pltpu.VMEM((ROWS, 1024), BF16),
            pltpu.VMEM((ROWS, 16), BF16),
            pltpu.VMEM((2, SEQ), jnp.int32),
            pltpu.VMEM((16, ROWS, 128), BF16),
            pltpu.VMEM((16, ROWS, 128), BF16),
            pltpu.VMEM((16, ROWS, 128), BF16),
            pltpu.VMEM((16, ROWS, 128), BF16),
            pltpu.VMEM((2, MEMBERS, ROWS, 128), BF16),
            pltpu.VMEM((8, ROWS, 256), BF16),
            pltpu.VMEM((8, ROWS, 256), BF16),
            pltpu.VMEM((8, ROWS, 256), BF16),
            pltpu.VMEM((8, ROWS, 256), BF16),
            pltpu.VMEM((ROWS, 128), F32),
            pltpu.VMEM((ROWS, 128), F32),
            pltpu.VMEM((ROWS, WIDTH // 2), BF16),
            pltpu.VMEM((MEMBERS, 16, WIDTH // 2), BF16),
            pltpu.VMEM((16, WIDTH // 2), BF16),
            pltpu.VMEM((16, WIDTH // 2), BF16),
            dma((3, 2)),
            dma((3, 2, 15)),
            dma((5,)),
            dma((16,)),
            dma((16,)),
            dma((16,)),
            dma((16,)),
            dma((16,)),
            dma((16,)),
            dma((8,)),
            dma((8,)),
            dma((3,)),
            dma((3,)),
            dma,
            dma,
        ],
        compiler_params=pltpu.CompilerParams(
            collective_id=0, has_side_effects=True, vmem_limit_bytes=58 * 1024 * 1024
        ),
        name="relay",
    )(
        hidden_input.reshape(ROWS, WIDTH),
        document_index[0],
        query_key_value_weight[0].reshape(256, 1536),
        output_weight[0],
        adapter_down[0, 0].T,
        adapter_up[0, 0],
        attention_gain[0],
        final_norm_gain,
        jnp.asarray(cosine),
        jnp.asarray(sine),
    )
    return averaged.reshape(1, 2, SEQ, WIDTH // 2)


def solution(mesh):
    return jax.shard_map(
        per_device,
        mesh=mesh,
        in_specs=(
            P("member", "section", None, None, None),
            P("section", None, None),
            P("section", "member", "tensor", None),
            P("section", "tensor", "member"),
            P("member", "section", "tensor", None),
            P("member", "section", None, None),
            P("member", "section", None),
            P("member", "tensor"),
        ),
        out_specs=P("section", None, None, "tensor"),
        check_vma=False,
    )
```

time: 512 us -> 186 us (0.36)
  waiting for transfers between devices: 398 us -> 0 us
  Pallas kernels: 0 us -> 178 us
  matrix products: 44.3 us -> 0 us
  local copies, waits for them, and re-layouts: 35 us -> 4.4 us
  other arithmetic: 14.6 us -> 0 us
  between operations: 13.3 us -> 0.01 us
    pallas_call x0 -> x1, Pallas kernels: none -> 178 us  [per_device(): pl.pallas_call(kernel, out_shape=jax.ShapeDtypeStruct((ROWS, WIDTH // 2),...]
    psum x3 -> x0, waiting for transfers between devices: 164 us -> none  [the longest x1 97 us: per_device(): lax.psum(normed_rows.astype(jnp.bfloat16), 'member').astype(jnp.float32)]
    all_gather x2 -> x0, waiting for transfers between devices: 134 us -> none  [the longest x1 92.8 us: per_device(): lax.all_gather(query_key_value_weight, 'member', axis=1, tiled=True)]
    ppermute x3 -> x0, waiting for transfers between devices: 97.8 us -> none  [shifted(): return lax.ppermute(block, axis, route)]
    dot_general x8 -> x0, matrix products: 42.7 us -> none  [the longest x2 15.3 us: per_device(): jnp.dot(context, out_full[0], preferred_element_type=jnp.float32)]
    another operation x1 -> x0, local copies, waits for them, and re-layouts: 31.2 us -> none  [per_device(): qkv_matrix = qkv_full[0].reshape(model_dim, -1)]
    convert_element_type x5 -> x0, other arithmetic: 8.35 us -> none  [the longest x2 6.03 us: per_device(): (hidden_f.reshape(token_count, model_dim) + summed).astype(jnp.bfloat16)]
  transfers between devices with their start and end apart: 8 -> 0, of which waited for: 8 -> 0; matrix products, arithmetic and copies ran while one was open for 9% -> 0% of each run, Pallas kernels for 0% -> 0%
where the time goes in v1:
time: 186 us; the launch traced here: 182 us
  Pallas kernels  178 us (96%)
  local copies, waits for them, and re-layouts  4.4 us (2%)
    pallas_call x1, Pallas kernels, per_device(): pl.pallas_call(kernel, out_shape=jax.ShapeDtypeStruct((ROWS, WIDTH // 2),...  178 us
    unnamed x2, local copies, waits for them, and re-layouts  4.4 us

profile of v1, /device:TPU:1, one launch (start us, length us, event | category | flops | bytes accessed | tf_op | source)
XLA Modules:
  0.0 182.4 jit_solution(1545268481589662861)
XLA Ops:
  0.0 2.1 %copy.11 = bf16[32,8,2,768]{3,1,2,0:T(8,128)(2,1)} copy(bf16[32,8,2,768]{3,2,1,0:T(2,128)(2,1)} %bitcast.15) | data formatting | bytes 1572864
  2.1 178.0 %relay.1 = bf16[256,2048]{1,0:T(8,128)(2,1)} custom-call(bf16[256,4096]{1,0:T(8,128)(2,1)} %bitcast.14, s32[2,128]{1,0:T(2,128)} %bitcast.20, bf16[256,1536]{1,0:T(8,128)(2,1)} %bitcast.13, bf16[1024,256]{1,0:T(8,128)(2,1)} %bitcast.16, bf16[16,1024]{1,0:T(8,128)(2,1)} %bitcast.18, bf16[16,4096]{1,0:T(8,128)(2,1)} %bitcast.17, f32[1,4096]{1,0:T(1,128)} %bitcast.19, ...), custom_call_target="tpu_custom_call" | custom-call | tf_op jit(solution)/shard_map/relay/pallas_call | solution.py:572
  180.1 2.3 %copy.13 = bf16[1,2,128,2048]{3,2,1,0:T(8,128)(2,1)} copy(bf16[1,2,128,2048]{3,2,1,0:T(8,128)(2,1)} %bitcast.12) | data formatting | bytes 2097152

commit v2 on v0

v2 whole, which is shorter than its diff:
```python
import math

import jax
import jax.numpy as jnp
import numpy as np
from jax import lax
from jax.experimental import pallas as pl
from jax.experimental.pallas import tpu as pltpu
from jax.sharding import PartitionSpec as P

HEAD_WIDTH = 128
GROUP = 4
WIDTH = 4096
ROWS = 256
SEQ = 128
MEMBERS = 16
SIDE = 4
EPS = 1e-05
MESH = pl.DeviceIdType.MESH
F32 = jnp.float32
BF16 = jnp.bfloat16


def rope_tables():
    position = np.arange(SEQ, dtype=np.float32)
    frequency = np.exp(
        np.arange(HEAD_WIDTH // 2, dtype=np.float32)
        * np.float32(-2.0 * math.log(500000.0) / HEAD_WIDTH)
    ).astype(np.float32)
    angles = (position[:, None] * frequency[None, :]).astype(np.float32)
    cosine, sine = np.cos(angles), np.sin(angles)
    return (
        np.concatenate([cosine, cosine], axis=1).astype(np.float32),
        np.concatenate([-sine, sine], axis=1).astype(np.float32),
    )


def wrap(value):
    return lax.rem(value + 2 * SIDE, SIDE)


class Torus:
    def __init__(self):
        self.member = lax.axis_index("member")
        self.x = lax.rem(self.member, SIDE)
        self.y = self.member // SIDE

    def at(self, part, du, dv):
        dx, dy = (du, dv) if part == 0 else (dv, du)
        return wrap(self.y + dy) * SIDE + wrap(self.x + dx)


class Place(Torus):
    def __init__(self):
        super().__init__()
        self.kind = lax.rem((self.x + 1) // 2, 2)
        self.parity = lax.rem(self.x, 2)
        self.pair_x = self.x + 1 - 2 * self.parity
        self.pair = self.y * SIDE + self.pair_x
        self.index = self.y * 2 + self.x // 2

    def column(self, f):
        return self.x + f * (3 - 2 * self.x)

    def row(self, dy):
        return wrap(self.y + dy)

    def near(self, f, dy):
        return self.row(dy) * SIDE + self.column(f)

    def pair_near(self, f, dy):
        return self.row(dy) * SIDE + self.pair_x + f * (3 - 2 * self.pair_x)


class PairGather:
    def __init__(self, place, own, slot, whole, send_sem, recv_sem):
        self.place, self.own, self.slot, self.whole = place, own, slot, whole
        self.send_sem, self.recv_sem = send_sem, recv_sem

    def copy(self, src, dst, part, f, dy, index):
        return pltpu.make_async_remote_copy(
            src_ref=src,
            dst_ref=dst,
            send_sem=self.send_sem.at[part],
            recv_sem=self.recv_sem.at[part, index],
            device_id={"member": self.place.near(f, dy)},
            device_id_type=MESH,
        )

    def ref(self, part, f, dy, which=None):
        return self.slot(self.place.column(f), self.place.row(dy), part, which)

    def move(self, part, f, dy, which, to_f, to_dy, index):
        ref = self.ref(part, f, dy, which)
        self.copy(ref, ref, part, to_f, to_dy, index).start()

    def wait(self, part, f, dy, index):
        ref = self.ref(part, f, dy)
        self.copy(ref, ref, part, 1, 0, index).wait_recv()

    def begin(self):
        for part, targets in ((0, ((1, 0), (0, 1), (0, -1))), (1, ((0, 1), (0, -1), (1, 0)))):
            for index, (f, dy) in enumerate(targets):
                self.copy(self.own(part), self.ref(part, 0, 0), part, f, dy, index).start()

    def middle(self):
        self.wait(0, 1, 0, 0)
        self.move(0, 1, 0, None, 0, 1, 3)
        self.move(0, 1, 0, None, 0, -1, 4)
        self.wait(1, 0, -1, 0)
        self.move(1, 0, -1, 0, 0, 1, 3)
        self.move(1, 0, -1, None, 1, 0, 4)
        self.wait(1, 0, 1, 1)
        self.move(1, 0, 1, 1, 0, -1, 3)
        self.move(1, 0, 1, None, 1, 0, 5)

    def late(self):
        self.wait(0, 0, -1, 1)
        self.move(0, 0, -1, 0, 0, 1, 5)
        self.wait(0, 0, 1, 2)
        self.move(0, 0, 1, 1, 0, -1, 5)
        self.wait(1, 0, 2, 3)
        self.move(1, 0, 2, None, 1, 0, 6)
        self.wait(0, 1, -1, 3)
        self.move(0, 1, -1, 0, 0, 1, 6)
        self.wait(0, 1, 1, 4)
        self.move(0, 1, 1, 1, 0, -1, 6)

    def end(self, stage):
        if stage == 0:
            self.wait(1, 1, 0, 2)
        elif stage == 1:
            self.wait(1, 1, -1, 4)
            self.wait(1, 1, 1, 5)
        elif stage == 2:
            self.wait(0, 0, 2, 5)
        else:
            self.wait(0, 1, 2, 6)
            self.wait(1, 1, 2, 6)

    def sent(self):
        for part in (0, 1):
            ref = self.whole(part)
            self.copy(ref, ref, part, 1, 0, 0).wait_send()


class Gather:
    order = (0, -1, 1, 2)

    def __init__(self, torus, own, slot, whole, send_sem, recv_sem):
        self.torus, self.own, self.slot, self.whole = torus, own, slot, whole
        self.send_sem, self.recv_sem = send_sem, recv_sem

    def start(self, src, dst, part, du, dv, index):
        pltpu.make_async_remote_copy(
            src_ref=src,
            dst_ref=dst,
            send_sem=self.send_sem.at[part],
            recv_sem=self.recv_sem.at[part, index],
            device_id={"member": self.torus.at(part, du, dv)},
            device_id_type=MESH,
        ).start()

    def wait(self, part, du, dv, index):
        ref = self.slot(part, self.torus.at(part, du, dv), None)
        pltpu.make_async_remote_copy(
            src_ref=ref,
            dst_ref=ref,
            send_sem=self.send_sem.at[part],
            recv_sem=self.recv_sem.at[part, index],
            device_id={"member": self.torus.at(part, 1, 0)},
            device_id_type=MESH,
        ).wait_recv()

    def full(self, part, du, dv):
        return self.slot(part, self.torus.at(part, du, dv), None)

    def half(self, part, du, dv, which):
        return self.slot(part, self.torus.at(part, du, dv), which)

    def spread(self, part, q):
        du = self.order[q]
        here = self.full(part, du, 0)
        src = self.own(part) if q == 0 else here
        self.start(src, here, part, 0, 1, 3 + q)
        self.start(src, here, part, 0, -1, 7 + q)

    def first(self, part):
        here = self.full(part, 0, 0)
        self.start(self.own(part), here, part, 1, 0, 0)
        self.start(self.own(part), here, part, -1, 0, 1)

    def line(self, part):
        self.wait(part, -1, 0, 0)
        ref = self.half(part, -1, 0, 0)
        self.start(ref, ref, part, 1, 0, 2)
        self.spread(part, 1)
        self.wait(part, 1, 0, 1)
        ref = self.half(part, 1, 0, 1)
        self.start(ref, ref, part, -1, 0, 2)
        self.spread(part, 2)

    def far(self, part):
        self.wait(part, 2, 0, 2)
        self.spread(part, 3)

    def cross(self, part, q):
        du = self.order[q]
        self.wait(part, du, -1, 3 + q)
        ref = self.half(part, du, -1, 0)
        self.start(ref, ref, part, 0, 1, 11 + q)
        self.wait(part, du, 1, 7 + q)
        ref = self.half(part, du, 1, 1)
        self.start(ref, ref, part, 0, -1, 11 + q)

    def last(self, part, q):
        self.wait(part, self.order[q], 2, 11 + q)

    def sent(self, part):
        ref = self.whole(part)
        pltpu.make_async_remote_copy(
            src_ref=ref,
            dst_ref=ref,
            send_sem=self.send_sem.at[part],
            recv_sem=self.recv_sem.at[part, 0],
            device_id={"member": self.torus.at(part, 1, 0)},
            device_id_type=MESH,
        ).wait_send()


def rotate(values, cosine, sine):
    return (values * cosine + pltpu.roll(values, HEAD_WIDTH // 2, 1) * sine).astype(BF16)


QKV_SPLIT = (((0, 144), (0, 80), (80, 64)), ((144, 112), (144, 64), (208, 48)))
OUT_SPLIT = (((0, 1152), (0, 576), (576, 576)), ((1152, 896), (1152, 448), (1600, 448)))


def cut(split, part, which):
    return split[part][0 if which is None else which + 1]


BLOCKS = ((0, 0), (1, 0), (0, -1), (0, 1), (1, -1), (1, 1), (0, 2), (1, 2))


def kernel(
    hidden_in, docs_in, qkv_in, out_in, down_in, up_in, gain_in, final_in, cos_ref, sin_ref,
    out_ref,
    wq, wo, h_all, nrm, proj, ctx_one, ctx_two, low, docs_next, gain_all, down_all, up_all, final_all,
    h_send, h_next, h_last, square, stat_own, stat_in, rows_out, rows_in, mean_own, mean_in, fin,
    pg_send, pg_recv, ag_send, ag_recv, local_sem, ctx_s, ctx_r, hop_s, hop_r, fwd_s, fwd_r,
    misc_s, misc_r, scatter_s, scatter_r,
):
    place = Place()
    member, kind, parity, index8 = place.member, place.kind, place.parity, place.index
    section = lax.axis_index("section")
    tensor = lax.axis_index("tensor")
    other = 1 - tensor
    sections = 8
    after = lax.rem(section + 1, sections)
    before = lax.rem(section + sections - 1, sections)
    both = (0, 1)

    barrier = pltpu.get_barrier_semaphore()

    def signal(device):
        pl.semaphore_signal(barrier, inc=1, device_id=device, device_id_type=MESH)

    def greet(i, carry):
        signal({"member": lax.rem(member + i, MEMBERS)})
        return carry

    lax.fori_loop(1, MEMBERS, greet, 0)
    signal({"tensor": other})
    signal({"member": place.pair, "tensor": other})
    for near in (after, before):
        signal({"section": near})
        signal({"section": near, "tensor": other})

    pending = []

    def local(src, dst, index):
        copy = pltpu.make_async_copy(src, dst, local_sem.at[index])
        copy.start()
        return copy

    def misc(src, dst, index, device):
        copy = pltpu.make_async_remote_copy(
            src, dst, misc_s.at[index], misc_r.at[index], device, MESH
        )
        pending.append(copy)
        return copy

    load_h = local(hidden_in, h_all.at[parity], 0)
    loads = [
        local(gain_in, gain_all.at[parity], 1),
        local(down_in, down_all.at[parity, tensor], 2),
        local(up_in, up_all.at[parity], 3),
        local(final_in, final_all.at[parity, tensor], 4),
        local(
            qkv_in.at[:, pl.ds(pl.multiple_of(kind * 768, 256), 768)],
            wq.at[pl.ds(pl.multiple_of(member * 256, 256), 256)],
            5,
        ),
    ]
    load_o = local(
        out_in.at[:, pl.ds(pl.multiple_of(tensor * 128, 128), 128)],
        wo.at[index8, pl.ds(pl.multiple_of(tensor * 1024, 1024), 1024)],
        6,
    )
    pl.semaphore_wait(barrier, MEMBERS - 1 + 6)

    def qkv_slot(of_pair):
        def slot(x, y, part, which):
            if of_pair:
                x = x + 1 - 2 * lax.rem(x, 2)
            lower, size = cut(QKV_SPLIT, part, which)
            return wq.at[pl.ds(pl.multiple_of((y * SIDE + x) * 256 + lower, 16), size)]

        return slot

    def own_qkv(part):
        lower, size = cut(QKV_SPLIT, part, None)
        return qkv_in.at[pl.ds(lower, size), pl.ds(pl.multiple_of(kind * 768, 256), 768)]

    def whole_qkv(part):
        return wq.at[pl.ds(0, 7 * cut(QKV_SPLIT, part, None)[1])]

    def out_slot(x, y, part, which):
        lower, size = cut(OUT_SPLIT, part, which)
        return wo.at[y * 2 + x // 2, pl.ds(lower, size)]

    def whole_out(part):
        return wo.at[pl.ds(0, 7), pl.ds(0, cut(OUT_SPLIT, part, None)[1])]

    wave_one = PairGather(place, own_qkv, qkv_slot(False), whole_qkv, pg_send.at[0], pg_recv.at[0])
    pair_slot = qkv_slot(True)
    wave_two = PairGather(
        place,
        lambda part: pair_slot(place.x, place.y, part, None),
        pair_slot,
        whole_qkv,
        pg_send.at[1],
        pg_recv.at[1],
    )
    wave_out = PairGather(
        place,
        lambda part: out_slot(place.x, place.y, part, None),
        out_slot,
        whole_out,
        pg_send.at[2],
        pg_recv.at[2],
    )

    to_pair = {"member": place.pair}
    to_pair_other = {"member": place.pair, "tensor": other}
    to_other = {"tensor": other}

    rows_of = lambda m: wq.at[pl.ds(pl.multiple_of(m * 256, 256), 256)]
    seed = misc(
        qkv_in.at[:, pl.ds(pl.multiple_of((1 - kind) * 768, 256), 768)], rows_of(member), 0, to_pair
    )
    seed.start()
    wave_one.begin()
    half_of = lambda a, t: h_all.at[a, pl.ds(pl.multiple_of(t * 128, 128), 128)]
    share_h = misc(
        hidden_in.at[pl.ds(pl.multiple_of(tensor * 128, 128), 128)], half_of(parity, tensor), 1, to_pair
    )
    share_h.start()
    share_out = misc(
        out_in.at[:, pl.ds(pl.multiple_of(other * 128, 128), 128)],
        wo.at[index8, pl.ds(pl.multiple_of(tensor * 1024, 1024), 1024)],
        2,
        to_other,
    )
    share_out.start()
    small = [misc(gain_in, gain_all.at[parity], 3, to_pair), misc(up_in, up_all.at[parity], 4, to_pair)]
    for k, device in enumerate((to_other, to_pair, to_pair_other)):
        small.append(misc(down_in, down_all.at[parity, tensor], 5 + k, device))
        small.append(misc(final_in, final_all.at[parity, tensor], 8 + k, device))
    small.append(misc(docs_in, docs_next, 11, {"section": after}))
    for copy in small:
        copy.start()
    load_h.wait()
    loads[0].wait()

    def norm_first(a):
        def block(i, carry):
            rows = pl.ds(pl.multiple_of(i * 16, 16), 16)
            h = h_all[a, rows, :].astype(F32)
            scale = lax.rsqrt(jnp.mean(h * h, axis=-1, keepdims=True) + EPS)
            nrm[pl.ds(pl.multiple_of(a * 256 + i * 16, 16), 16), :] = (
                h * scale * gain_all[a]
            ).astype(BF16)
            return carry

        lax.fori_loop(0, ROWS // 16, block, 0)

    norm_first(parity)

    def project():
        def block(n, carry):
            rows = pl.ds(pl.multiple_of(lax.rem(n, 2) * 256, 256), 256)
            columns = pl.ds(pl.multiple_of(n // 2 * 256, 256), 256)
            proj[rows, columns] = jnp.dot(nrm[rows, :], wq[:, columns], preferred_element_type=F32)
            return carry

        lax.fori_loop(0, 6, block, 0)

    ahead = lax.broadcasted_iota(jnp.int32, (SEQ, SEQ), 0) >= lax.broadcasted_iota(
        jnp.int32, (SEQ, SEQ), 1
    )
    head = 2 * tensor + kind

    def ctx_copy(ctx, tick, s, which):
        owner = 2 * tensor + (1 - kind if which == 2 else kind)
        ref = ctx.at[
            pl.ds(pl.multiple_of(s * SEQ, SEQ), SEQ), pl.ds(pl.multiple_of(owner * 512, 512), 512)
        ]
        return pltpu.make_async_remote_copy(
            ref, ref, ctx_s.at[tick, which, s], ctx_r.at[tick, which, s],
            to_pair if which == 1 else to_other, MESH,
        )

    def ctx_arrived(ctx, tick, s, which):
        t = tensor if which == 1 else other
        owner = 2 * t + (kind if which == 0 else 1 - kind)
        ref = ctx.at[
            pl.ds(pl.multiple_of(s * SEQ, SEQ), SEQ), pl.ds(pl.multiple_of(owner * 512, 512), 512)
        ]
        pltpu.make_async_remote_copy(
            ref, ref, ctx_s.at[tick, which, s], ctx_r.at[tick, which, s], to_other, MESH
        ).wait_recv()

    def attend(docs_ref, ctx, tick):
        def sequence(s, carry):
            rows = pl.ds(pl.multiple_of(s * SEQ, SEQ), SEQ)
            numbers = docs_ref[pl.ds(lax.rem(s, 2), 1), :]
            numbers = jnp.broadcast_to(numbers, (SEQ, SEQ)).astype(F32)
            allowed = ahead & (numbers == numbers.T)
            allowed = jnp.concatenate([allowed.astype(F32)] * GROUP, axis=0) > 0.5
            cosine, sine = cos_ref[...], sin_ref[...]

            def piece(g):
                return proj[rows, g * 128 : g * 128 + 128]

            queries = jnp.concatenate(
                [rotate(piece(g), cosine, sine) for g in range(GROUP)], axis=0
            )
            keys = rotate(piece(GROUP), cosine, sine)
            values = piece(GROUP + 1).astype(BF16)
            scores = lax.dot_general(
                queries, keys, (((1,), (1,)), ((), ())), preferred_element_type=F32
            ) * (1.0 / math.sqrt(HEAD_WIDTH))
            scores = jnp.where(allowed, scores, -1e30)
            weights = jnp.exp(scores - jnp.max(scores, axis=-1, keepdims=True))
            weights = (weights / jnp.sum(weights, axis=-1, keepdims=True)).astype(BF16)
            context = jnp.dot(weights, values, preferred_element_type=F32).astype(BF16)
            for g in range(GROUP):
                columns = pl.ds(pl.multiple_of(head * 512 + g * 128, 128), 128)
                ctx[rows, columns] = context[g * SEQ : (g + 1) * SEQ]
            ctx_copy(ctx, tick, s, 1).start()
            ctx_copy(ctx, tick, s, 0).start()
            return carry

        lax.fori_loop(0, 4, sequence, 0)

    def collect(ctx, tick, a):
        for s in (2 * a, 2 * a + 1):
            ctx_arrived(ctx, tick, s, 1)
            ctx_copy(ctx, tick, s, 2).start()
        for s in (2 * a, 2 * a + 1):
            ctx_arrived(ctx, tick, s, 0)
            ctx_arrived(ctx, tick, s, 2)
        for block in both:
            low[a, block] = lax.dot_general(
                ctx[a * 256 : a * 256 + 256, block * 1024 : block * 1024 + 1024],
                down_all[a, block],
                (((1,), (1,)), ((), ())),
                preferred_element_type=F32,
            ).astype(BF16)

    wave_one.middle()
    seed_in = pltpu.make_async_remote_copy(
        rows_of(place.pair), rows_of(place.pair), misc_s.at[0], misc_r.at[0], to_pair, MESH
    )
    seed_in.wait_recv()
    wave_two.begin()
    wave_one.late()
    pltpu.make_async_remote_copy(
        half_of(1 - parity, tensor), half_of(1 - parity, tensor), misc_s.at[1], misc_r.at[1],
        to_pair, MESH,
    ).wait_recv()
    pass_h = misc(half_of(1 - parity, tensor), half_of(1 - parity, tensor), 12, to_other)
    pass_h.start()
    wave_two.middle()
    load_o.wait()
    share_in = wo.at[index8, pl.ds(pl.multiple_of(other * 1024, 1024), 1024)]
    pltpu.make_async_remote_copy(
        share_in, share_in, misc_s.at[2], misc_r.at[2], to_other, MESH
    ).wait_recv()
    wave_out.begin()
    pltpu.make_async_remote_copy(
        half_of(1 - parity, other), half_of(1 - parity, other), misc_s.at[12], misc_r.at[12],
        to_other, MESH,
    ).wait_recv()
    small[0].wait_recv()
    norm_first(1 - parity)
    wave_two.late()
    for copy in small[1:]:
        copy.wait_recv()
    for copy in loads[1:]:
        copy.wait()
    for stage in range(4):
        wave_one.end(stage)
        wave_two.end(stage)
    project()
    wave_out.middle()
    attend(docs_in, ctx_one, 0)
    wave_out.late()

    def block_member(i, pair=False):
        f, dy = BLOCKS[i]
        return place.pair_near(f, dy) if pair else place.near(f, dy)

    def columns_of(m):
        return pl.ds(pl.multiple_of(m * 256 + tensor * 128, 128), 128)

    def summed(ctx, a, weights_of, up):
        total = None
        for block in both:
            main = jnp.dot(
                ctx[a * 256 : a * 256 + 256, block * 1024 : block * 1024 + 1024],
                weights_of(block),
                preferred_element_type=F32,
            )
            value = main + jnp.dot(low[a, block], up, preferred_element_type=F32)
            value = value.astype(BF16).astype(F32)
            total = value if total is None else total + value
        return total

    def block_copy(ref, dst, kind_of, n, device):
        send, recv = (hop_s.at[n], hop_r.at[n]) if kind_of == 3 else (
            fwd_s.at[kind_of, n], fwd_r.at[kind_of, n]
        )
        return pltpu.make_async_remote_copy(ref, dst, send, recv, device, MESH)

    steps = [(i, 0) for i in range(4)] + [(i, 1) for i in range(4)]
    for i in range(4, 8):
        steps += [(i, 0), (i, 1)]

    def own_ref(n):
        i, a = steps[n]
        return h_next.at[block_member(i) * 2 + tensor, a]

    def hop_copy(n):
        return block_copy(h_send.at[n], own_ref(n), 3, n, {"section": after})

    def start_block(n):
        i, a = steps[n]
        f, dy = BLOCKS[i]
        slot = place.row(dy) * 2 + place.column(f) // 2
        columns = columns_of(block_member(i))
        total = summed(
            ctx_one, a, lambda block: wo[slot, block * 1024 : block * 1024 + 1024],
            up_all[a, :, columns],
        )
        h_send[n] = (h_all[a, :, columns].astype(F32) + total).astype(BF16)
        hop_copy(n).start()

    def pair_ref(n):
        i, a = steps[n]
        return h_next.at[block_member(i, True) * 2 + tensor, a]

    def pass_own(n, device, kind_of):
        return block_copy(own_ref(n), own_ref(n), kind_of, n, device)

    def pass_pair(n):
        return block_copy(pair_ref(n), pair_ref(n), 2, n, to_other)

    def arrive(n):
        hop_copy(n).wait_recv()
        pass_own(n, to_pair, 0).start()
        pass_own(n, to_other, 1).start()

    def relay(n):
        block_copy(pair_ref(n), pair_ref(n), 0, n, to_pair).wait_recv()
        pass_pair(n).start()

    def other_ref(n, pair):
        i, a = steps[n]
        return h_next.at[block_member(i, pair) * 2 + other, a]

    def run(lower, upper):
        for n in range(lower, upper):
            start_block(n)
            if n >= 2:
                arrive(n - 2)
            if n >= 5:
                relay(n - 5)

    collect(ctx_one, 0, 0)
    wave_out.end(0)
    run(0, 4)
    collect(ctx_one, 0, 1)
    run(4, 8)
    wave_out.end(1)
    run(8, 12)
    wave_out.end(2)
    run(12, 14)
    wave_out.end(3)
    run(14, 16)
    for n in (14, 15):
        arrive(n)
    for n in range(11, 16):
        relay(n)
    for n in range(16):
        ref = other_ref(n, False)
        block_copy(ref, ref, 1, n, to_other).wait_recv()
        ref = other_ref(n, True)
        block_copy(ref, ref, 2, n, to_other).wait_recv()

    def norm_second(i, carry):
        a = i // 8
        rows = pl.ds(pl.multiple_of(lax.rem(i, 8) * 32, 32), 32)
        total = jnp.zeros((32, 128), F32)
        for block in range(32):
            h = h_next[block, a, rows, :].astype(F32)
            total = total + h * h
        scale = lax.rsqrt(jnp.sum(total, axis=-1, keepdims=True) * (1.0 / WIDTH) + EPS)
        scale = jnp.broadcast_to(scale, (32, 128))
        for block in range(32):
            columns = slice(block * 128, block * 128 + 128)
            h = h_next[block, a, rows, :].astype(F32)
            nrm[pl.ds(pl.multiple_of(i * 32, 32), 32), columns] = (
                h * scale * gain_all[a, :, columns]
            ).astype(BF16)
        return carry

    lax.fori_loop(0, 16, norm_second, 0)
    project()
    attend(docs_next, ctx_two, 1)

    def pair_members(y):
        return y * SIDE + kind, y * SIDE + 3 - kind

    def pair_columns(ref, a, y, half):
        parts = []
        for m in pair_members(y):
            lower = (m - half * 8) * 256 + tensor * 128
            parts.append(ref[a, :, pl.ds(pl.multiple_of(lower, 128), 128)])
        return jnp.concatenate(parts, axis=1)

    for a in both:
        collect(ctx_two, 1, a)
        square[a] = jnp.zeros((ROWS, 128), F32)

        def last_block(y, carry):
            total = summed(
                ctx_two,
                a,
                lambda block: jnp.concatenate(
                    [wo[2 * y + k, block * 1024 : block * 1024 + 1024] for k in both], axis=1
                ),
                pair_columns(up_all, a, y, 0),
            )
            for k, m in enumerate(pair_members(y)):
                columns = slice(k * 128, k * 128 + 128)
                h = h_next[m * 2 + tensor, a].astype(F32) + total[:, columns]
                h = h.astype(BF16)
                h_last[a, y, :, columns] = h
                h = h.astype(F32)
                square[a] += h * h
            return carry

        lax.fori_loop(0, SIDE, last_block, 0)

    stat_own[...] = jnp.zeros_like(stat_own)
    for a in both:
        for r in both:
            stat_own[2 * a + r : 2 * a + r + 1, :] = jnp.sum(
                square[a, r * 128 : r * 128 + 128].T, axis=0, keepdims=True
            )
    stats = [
        misc(stat_own, stat_in.at[k], 13 + k, device)
        for k, device in enumerate((to_other, to_pair, to_pair_other))
    ]
    for copy in stats:
        copy.start()
    for copy in stats:
        copy.wait_recv()
    total = stat_own[...] + stat_in[0] + stat_in[1] + stat_in[2]
    scales = lax.rsqrt(total * (1.0 / WIDTH) + EPS)
    column_scale = [jnp.broadcast_to(scales[s : s + 1], (128, 128)).T for s in range(4)]
    for y in range(SIDE):
        for k, m in enumerate((y * SIDE + kind, y * SIDE + 3 - kind)):
            lower = (m - (y // 2) * 8) * 256 + tensor * 128
            gains = [
                final_all[a, y // 2, :, pl.ds(pl.multiple_of(lower, 128), 128)] for a in both
            ]
            columns = slice(k * 128, k * 128 + 128)
            for r in both:
                rows = slice(r * 128, r * 128 + 128)
                value = sum(
                    h_last[a, y, rows, columns].astype(F32) * column_scale[2 * a + r] * gains[a]
                    for a in both
                )
                rows_out[rows, (2 * y + k) * 128 : (2 * y + k + 1) * 128] = value.astype(BF16)

    def rows_at(i):
        return rows_out.at[pl.ds(pl.multiple_of(i * 32, 32), 32)]

    def scatter(i, carry):
        f, dy = lax.rem(i, 2), i // 2
        x, y = place.column(f), place.row(dy)
        pltpu.make_async_remote_copy(
            rows_at(y * 2 + x // 2), rows_in.at[index8], scatter_s, scatter_r,
            {"member": y * SIDE + x}, MESH,
        ).start()
        return carry

    lax.fori_loop(1, 8, scatter, 0)
    keep = local(rows_at(index8), rows_in.at[index8], 7)
    keep.wait()
    seven = pltpu.make_async_remote_copy(
        rows_in.at[pl.ds(0, 7)], rows_in.at[pl.ds(0, 7)], scatter_s, scatter_r, to_other, MESH
    )
    seven.wait_recv()
    total = rows_in[0].astype(F32)
    for i in range(1, 8):
        total = total + rows_in[i].astype(F32)
    total = (total * (1.0 / MEMBERS)).astype(BF16)
    for half in both:
        mean_own[half] = total[:, half * 512 : half * 512 + 512]
    hops = [
        misc(mean_own.at[tensor], mean_in.at[tensor], 16, {"section": after}),
        misc(mean_own.at[other], mean_in.at[tensor], 17, {"section": after, "tensor": other}),
    ]
    for copy in hops:
        copy.start()
    hops[0].wait_recv()
    pltpu.make_async_remote_copy(
        mean_own.at[other], mean_in.at[other], misc_s.at[17], misc_r.at[17],
        {"section": after, "tensor": other}, MESH,
    ).wait_recv()

    def mean_slot(part, slot, which):
        if which is None:
            return fin.at[slot, part]
        return fin.at[slot, part, :, pl.ds(which * 256, 256)]

    final = Gather(
        place,
        lambda part: mean_in.at[part],
        mean_slot,
        lambda part: fin.at[pl.ds(0, 15), part],
        ag_send,
        ag_recv,
    )
    for part in both:
        final.first(part)
    for part in both:
        final.spread(part, 0)
    fin[member] = mean_in[...]
    for part in both:
        final.line(part)
    for part in both:
        final.cross(part, 0)
    for part in both:
        final.far(part)
    for q in (1, 2, 3):
        for part in both:
            final.cross(part, q)
    for q in range(SIDE):
        for part in both:
            final.last(part, q)
    for m in range(MEMBERS):
        x, y = m % SIDE, m // SIDE
        side = ((x + 1) // 2) % 2
        rows = slice((y * 2 + x // 2) * 32, (y * 2 + x // 2) * 32 + 32)
        for part in both:
            for s in range(4):
                column = (s // 2 * SIDE + (side if s % 2 == 0 else 3 - side)) * 256 + part * 128
                out_ref[rows, column : column + 128] = fin[m, part, :, s * 128 : s * 128 + 128]

    for wave in (wave_one, wave_two, wave_out):
        wave.sent()
    for part in both:
        final.sent(part)
    for tick, ctx in enumerate((ctx_one, ctx_two)):
        for which in range(3):
            for s in range(4):
                ctx_copy(ctx, tick, s, which).wait_send()
    for n in range(16):
        hop_copy(n).wait_send()
        pass_own(n, to_pair, 0).wait_send()
        pass_own(n, to_other, 1).wait_send()
        pass_pair(n).wait_send()
    for copy in pending:
        copy.wait_send()
    seven.wait_send()


def per_device(
    hidden_input,
    document_index,
    query_key_value_weight,
    output_weight,
    adapter_down,
    adapter_up,
    attention_gain,
    final_norm_gain,
):
    cosine, sine = rope_tables()
    vmem = pl.BlockSpec(memory_space=pltpu.VMEM)
    anywhere = pl.BlockSpec(memory_space=pl.ANY)
    dma = pltpu.SemaphoreType.DMA
    averaged = pl.pallas_call(
        kernel,
        out_shape=jax.ShapeDtypeStruct((ROWS, WIDTH // 2), BF16),
        in_specs=[anywhere, vmem, anywhere, anywhere] + [vmem] * 6,
        out_specs=vmem,
        scratch_shapes=[
            pltpu.VMEM((WIDTH, 768), BF16),
            pltpu.VMEM((8, 2048, 128), BF16),
            pltpu.VMEM((2, ROWS, WIDTH), BF16),
            pltpu.VMEM((2 * ROWS, WIDTH), BF16),
            pltpu.VMEM((2 * ROWS, 768), F32),
            pltpu.VMEM((2 * ROWS, 2048), BF16),
            pltpu.VMEM((2 * ROWS, 2048), BF16),
            pltpu.VMEM((2, 2, ROWS, 16), BF16),
            pltpu.VMEM((2, SEQ), jnp.int32),
            pltpu.VMEM((2, 1, WIDTH), F32),
            pltpu.VMEM((2, 2, 16, 1024), BF16),
            pltpu.VMEM((2, 16, WIDTH), BF16),
            pltpu.VMEM((2, 2, 1, WIDTH // 2), F32),
            pltpu.VMEM((16, ROWS, 128), BF16),
            pltpu.VMEM((32, 2, ROWS, 128), BF16),
            pltpu.VMEM((2, SIDE, ROWS, 256), BF16),
            pltpu.VMEM((2, ROWS, 128), F32),
            pltpu.VMEM((8, 128), F32),
            pltpu.VMEM((3, 8, 128), F32),
            pltpu.VMEM((ROWS, 1024), BF16),
            pltpu.VMEM((8, 32, 1024), BF16),
            pltpu.VMEM((2, 32, 512), BF16),
            pltpu.VMEM((2, 32, 512), BF16),
            pltpu.VMEM((MEMBERS, 2, 32, 512), BF16),
            dma((3, 2)),
            dma((3, 2, 7)),
            dma((2,)),
            dma((2, 15)),
            dma((8,)),
            dma((2, 3, 4)),
            dma((2, 3, 4)),
            dma((16,)),
            dma((16,)),
            dma((3, 16)),
            dma((3, 16)),
            dma((18,)),
            dma((18,)),
            dma,
            dma,
        ],
        compiler_params=pltpu.CompilerParams(
            collective_id=0, has_side_effects=True, vmem_limit_bytes=58 * 1024 * 1024
        ),
        name="relay",
    )(
        hidden_input.reshape(ROWS, WIDTH),
        document_index[0],
        query_key_value_weight[0].reshape(256, 1536),
        output_weight[0],
        adapter_down[0, 0].T,
        adapter_up[0, 0],
        attention_gain[0],
        final_norm_gain,
        jnp.asarray(cosine),
        jnp.asarray(sine),
    )
    return averaged.reshape(1, 2, SEQ, WIDTH // 2)


def solution(mesh):
    return jax.shard_map(
        per_device,
        mesh=mesh,
        in_specs=(
            P("member", "section", None, None, None),
            P("section", None, None),
            P("section", "member", "tensor", None),
            P("section", "tensor", "member"),
            P("member", "section", "tensor", None),
            P("member", "section", None, None),
            P("member", "section", None),
            P("member", "tensor"),
        ),
        out_specs=P("section", None, None, "tensor"),
        check_vma=False,
    )
```

time: 512 us -> 178 us (0.35)
  waiting for transfers between devices: 398 us -> 0 us
  Pallas kernels: 0 us -> 172 us
  matrix products: 44.3 us -> 0 us
  local copies, waits for them, and re-layouts: 35 us -> 4.4 us
  other arithmetic: 14.6 us -> 0 us
  between operations: 13.3 us -> 0.01 us
    pallas_call x0 -> x1, Pallas kernels: none -> 172 us  [per_device(): pl.pallas_call(kernel, out_shape=jax.ShapeDtypeStruct((ROWS, WIDTH // 2),...]
    psum x3 -> x0, waiting for transfers between devices: 164 us -> none  [the longest x1 97 us: per_device(): lax.psum(normed_rows.astype(jnp.bfloat16), 'member').astype(jnp.float32)]
    all_gather x2 -> x0, waiting for transfers between devices: 134 us -> none  [the longest x1 92.8 us: per_device(): lax.all_gather(query_key_value_weight, 'member', axis=1, tiled=True)]
    ppermute x3 -> x0, waiting for transfers between devices: 97.8 us -> none  [shifted(): return lax.ppermute(block, axis, route)]
    dot_general x8 -> x0, matrix products: 42.7 us -> none  [the longest x2 15.3 us: per_device(): jnp.dot(context, out_full[0], preferred_element_type=jnp.float32)]
    another operation x1 -> x0, local copies, waits for them, and re-layouts: 31.2 us -> none  [per_device(): qkv_matrix = qkv_full[0].reshape(model_dim, -1)]
    convert_element_type x5 -> x0, other arithmetic: 8.35 us -> none  [the longest x2 6.03 us: per_device(): (hidden_f.reshape(token_count, model_dim) + summed).astype(jnp.bfloat16)]
  transfers between devices with their start and end apart: 8 -> 0, of which waited for: 8 -> 0; matrix products, arithmetic and copies ran while one was open for 9% -> 0% of each run, Pallas kernels for 0% -> 0%
where the time goes in v2:
time: 178 us; the launch traced here: 176 us
  Pallas kernels  172 us (97%)
  local copies, waits for them, and re-layouts  4.4 us (2%)
    pallas_call x1, Pallas kernels, per_device(): pl.pallas_call(kernel, out_shape=jax.ShapeDtypeStruct((ROWS, WIDTH // 2),...  172 us
    unnamed x2, local copies, waits for them, and re-layouts  4.4 us

profile of v2, /device:TPU:1, one launch (start us, length us, event | category | flops | bytes accessed | tf_op | source)
XLA Modules:
  0.0 176.2 jit_solution(753487919486064679)
XLA Ops:
  0.0 2.1 %copy.11 = bf16[32,8,2,768]{3,1,2,0:T(8,128)(2,1)} copy(bf16[32,8,2,768]{3,2,1,0:T(2,128)(2,1)} %bitcast.15) | data formatting | bytes 1572864
  2.1 171.8 %relay.1 = bf16[256,2048]{1,0:T(8,128)(2,1)} custom-call(bf16[256,4096]{1,0:T(8,128)(2,1)} %bitcast.14, s32[2,128]{1,0:T(2,128)} %bitcast.20, bf16[256,1536]{1,0:T(8,128)(2,1)} %bitcast.13, bf16[1024,256]{1,0:T(8,128)(2,1)} %bitcast.16, bf16[16,1024]{1,0:T(8,128)(2,1)} %bitcast.18, bf16[16,4096]{1,0:T(8,128)(2,1)} %bitcast.17, f32[1,4096]{1,0:T(1,128)} %bitcast.19, ...), custom_call_target="tpu_custom_call" | custom-call | tf_op jit(solution)/shard_map/relay/pallas_call | solution.py:818
  173.9 2.3 %copy.13 = bf16[1,2,128,2048]{3,2,1,0:T(8,128)(2,1)} copy(bf16[1,2,128,2048]{3,2,1,0:T(8,128)(2,1)} %bitcast.12) | data formatting | bytes 2097152

commit v3 on v2

--- a/solution.py
+++ b/solution.py
@@ -144,88 +144,59 @@
             self.copy(ref, ref, part, 1, 0, 0).wait_send()
 
 
-class Gather:
+class PlaneGather:
     order = (0, -1, 1, 2)
 
     def __init__(self, torus, own, slot, whole, send_sem, recv_sem):
         self.torus, self.own, self.slot, self.whole = torus, own, slot, whole
         self.send_sem, self.recv_sem = send_sem, recv_sem
 
-    def start(self, src, dst, part, du, dv, index):
-        pltpu.make_async_remote_copy(
+    def copy(self, src, dst, part, du, dv, index):
+        return pltpu.make_async_remote_copy(
             src_ref=src,
             dst_ref=dst,
             send_sem=self.send_sem.at[part],
             recv_sem=self.recv_sem.at[part, index],
             device_id={"member": self.torus.at(part, du, dv)},
             device_id_type=MESH,
-        ).start()
+        )
+
+    def ref(self, part, du, dv):
+        return self.slot(part, self.torus.at(part, du, dv))
+
+    def begin(self):
+        for part in (0, 1):
+            for k in (1, 2, 3):
+                self.copy(self.own(part), self.ref(part, 0, 0), part, -self.order[k], 0, k - 1).start()
+        for part in (0, 1):
+            self.spread(part, 0)
+
+    def spread(self, part, q):
+        here = self.ref(part, self.order[q], 0)
+        src = self.own(part) if q == 0 else here
+        for k in (1, 2, 3):
+            self.copy(src, here, part, 0, -self.order[k], 3 * q + k + 2).start()
 
     def wait(self, part, du, dv, index):
-        ref = self.slot(part, self.torus.at(part, du, dv), None)
-        pltpu.make_async_remote_copy(
-            src_ref=ref,
-            dst_ref=ref,
-            send_sem=self.send_sem.at[part],
-            recv_sem=self.recv_sem.at[part, index],
-            device_id={"member": self.torus.at(part, 1, 0)},
-            device_id_type=MESH,
-        ).wait_recv()
-
-    def full(self, part, du, dv):
-        return self.slot(part, self.torus.at(part, du, dv), None)
-
-    def half(self, part, du, dv, which):
-        return self.slot(part, self.torus.at(part, du, dv), which)
-
-    def spread(self, part, q):
-        du = self.order[q]
-        here = self.full(part, du, 0)
-        src = self.own(part) if q == 0 else here
-        self.start(src, here, part, 0, 1, 3 + q)
-        self.start(src, here, part, 0, -1, 7 + q)
-
-    def first(self, part):
-        here = self.full(part, 0, 0)
-        self.start(self.own(part), here, part, 1, 0, 0)
-        self.start(self.own(part), here, part, -1, 0, 1)
-
-    def line(self, part):
-        self.wait(part, -1, 0, 0)
-        ref = self.half(part, -1, 0, 0)
-        self.start(ref, ref, part, 1, 0, 2)
-        self.spread(part, 1)
-        self.wait(part, 1, 0, 1)
-        ref = self.half(part, 1, 0, 1)
-        self.start(ref, ref, part, -1, 0, 2)
-        self.spread(part, 2)
-
-    def far(self, part):
-        self.wait(part, 2, 0, 2)
-        self.spread(part, 3)
-
-    def cross(self, part, q):
-        du = self.order[q]
-        self.wait(part, du, -1, 3 + q)
-        ref = self.half(part, du, -1, 0)
-        self.start(ref, ref, part, 0, 1, 11 + q)
-        self.wait(part, du, 1, 7 + q)
-        ref = self.half(part, du, 1, 1)
-        self.start(ref, ref, part, 0, -1, 11 + q)
-
-    def last(self, part, q):
-        self.wait(part, self.order[q], 2, 11 + q)
-
-    def sent(self, part):
-        ref = self.whole(part)
-        pltpu.make_async_remote_copy(
-            src_ref=ref,
-            dst_ref=ref,
-            send_sem=self.send_sem.at[part],
-            recv_sem=self.recv_sem.at[part, 0],
-            device_id={"member": self.torus.at(part, 1, 0)},
-            device_id_type=MESH,
-        ).wait_send()
+        ref = self.ref(part, du, dv)
+        self.copy(ref, ref, part, 1, 0, index).wait_recv()
+
+    def middle(self):
+        for q in (1, 2, 3):
+            for part in (0, 1):
+                self.wait(part, self.order[q], 0, q - 1)
+                self.spread(part, q)
+
+    def end(self):
+        for q in range(SIDE):
+            for part in (0, 1):
+                for k in (1, 2, 3):
+                    self.wait(part, self.order[q], self.order[k], 3 * q + k + 2)
+
+    def sent(self):
+        for part in (0, 1):
+            ref = self.whole(part)
+            self.copy(ref, ref, part, 1, 0, 0).wait_send()
 
 
 def rotate(values, cosine, sine):
@@ -291,7 +262,7 @@
         pending.append(copy)
         return copy
 
-    load_h = local(hidden_in, h_all.at[parity], 0)
+    load_h = local(hidden_in, h_all.at[:, parity], 0)
     loads = [
         local(gain_in, gain_all.at[parity], 1),
         local(down_in, down_all.at[parity, tensor], 2),
@@ -362,9 +333,9 @@
     )
     seed.start()
     wave_one.begin()
-    half_of = lambda a, t: h_all.at[a, pl.ds(pl.multiple_of(t * 128, 128), 128)]
+    half_of = lambda a, t: h_all.at[t, a]
     share_h = misc(
-        hidden_in.at[pl.ds(pl.multiple_of(tensor * 128, 128), 128)], half_of(parity, tensor), 1, to_pair
+        hidden_in.at[tensor], half_of(parity, tensor), 1, to_pair
     )
     share_h.start()
     share_out = misc(
@@ -386,10 +357,10 @@
 
     def norm_first(a):
         def block(i, carry):
-            rows = pl.ds(pl.multiple_of(i * 16, 16), 16)
-            h = h_all[a, rows, :].astype(F32)
+            r, j = i // 8, lax.rem(i, 8)
+            h = h_all[r, a, pl.ds(pl.multiple_of(j * 16, 16), 16), :].astype(F32)
             scale = lax.rsqrt(jnp.mean(h * h, axis=-1, keepdims=True) + EPS)
-            nrm[pl.ds(pl.multiple_of(a * 256 + i * 16, 16), 16), :] = (
+            nrm[pl.ds(pl.multiple_of(r * 256 + a * 128 + j * 16, 16), 16), :] = (
                 h * scale * gain_all[a]
             ).astype(BF16)
             return carry
@@ -398,14 +369,14 @@
 
     norm_first(parity)
 
-    def project():
+    def project(lower, upper):
         def block(n, carry):
-            rows = pl.ds(pl.multiple_of(lax.rem(n, 2) * 256, 256), 256)
-            columns = pl.ds(pl.multiple_of(n // 2 * 256, 256), 256)
+            rows = pl.ds(pl.multiple_of(n // 3 * 256, 256), 256)
+            columns = pl.ds(pl.multiple_of(lax.rem(n, 3) * 256, 256), 256)
             proj[rows, columns] = jnp.dot(nrm[rows, :], wq[:, columns], preferred_element_type=F32)
             return carry
 
-        lax.fori_loop(0, 6, block, 0)
+        lax.fori_loop(lower, upper, block, 0)
 
     ahead = lax.broadcasted_iota(jnp.int32, (SEQ, SEQ), 0) >= lax.broadcasted_iota(
         jnp.int32, (SEQ, SEQ), 1
@@ -432,10 +403,10 @@
             ref, ref, ctx_s.at[tick, which, s], ctx_r.at[tick, which, s], to_other, MESH
         ).wait_recv()
 
-    def attend(docs_ref, ctx, tick):
+    def attend(docs_ref, ctx, tick, lower, upper):
         def sequence(s, carry):
             rows = pl.ds(pl.multiple_of(s * SEQ, SEQ), SEQ)
-            numbers = docs_ref[pl.ds(lax.rem(s, 2), 1), :]
+            numbers = docs_ref[pl.ds(s // 2, 1), :]
             numbers = jnp.broadcast_to(numbers, (SEQ, SEQ)).astype(F32)
             allowed = ahead & (numbers == numbers.T)
             allowed = jnp.concatenate([allowed.astype(F32)] * GROUP, axis=0) > 0.5
@@ -463,22 +434,24 @@
             ctx_copy(ctx, tick, s, 0).start()
             return carry
 
-        lax.fori_loop(0, 4, sequence, 0)
-
-    def collect(ctx, tick, a):
-        for s in (2 * a, 2 * a + 1):
-            ctx_arrived(ctx, tick, s, 1)
-            ctx_copy(ctx, tick, s, 2).start()
-        for s in (2 * a, 2 * a + 1):
-            ctx_arrived(ctx, tick, s, 0)
-            ctx_arrived(ctx, tick, s, 2)
-        for block in both:
-            low[a, block] = lax.dot_general(
-                ctx[a * 256 : a * 256 + 256, block * 1024 : block * 1024 + 1024],
-                down_all[a, block],
-                (((1,), (1,)), ((), ())),
-                preferred_element_type=F32,
-            ).astype(BF16)
+        lax.fori_loop(lower, upper, sequence, 0)
+
+    def collect(ctx, tick, r):
+        for a in both:
+            ctx_arrived(ctx, tick, 2 * r + a, 1)
+            ctx_copy(ctx, tick, 2 * r + a, 2).start()
+        for a in both:
+            ctx_arrived(ctx, tick, 2 * r + a, 0)
+            ctx_arrived(ctx, tick, 2 * r + a, 2)
+        for a in both:
+            rows = slice((2 * r + a) * SEQ, (2 * r + a + 1) * SEQ)
+            for block in both:
+                low[block, rows] = lax.dot_general(
+                    ctx[rows, block * 1024 : block * 1024 + 1024],
+                    down_all[a, block],
+                    (((1,), (1,)), ((), ())),
+                    preferred_element_type=F32,
+                ).astype(BF16)
 
     wave_one.middle()
     seed_in = pltpu.make_async_remote_copy(
@@ -499,14 +472,14 @@
     pltpu.make_async_remote_copy(
         share_in, share_in, misc_s.at[2], misc_r.at[2], to_other, MESH
     ).wait_recv()
-    wave_out.begin()
+    wave_two.late()
     pltpu.make_async_remote_copy(
         half_of(1 - parity, other), half_of(1 - parity, other), misc_s.at[12], misc_r.at[12],
         to_other, MESH,
     ).wait_recv()
     small[0].wait_recv()
     norm_first(1 - parity)
-    wave_two.late()
+    wave_out.begin()
     for copy in small[1:]:
         copy.wait_recv()
     for copy in loads[1:]:
@@ -514,9 +487,11 @@
     for stage in range(4):
         wave_one.end(stage)
         wave_two.end(stage)
-    project()
+    project(0, 3)
+    attend(docs_in, ctx_one, 0, 0, 2)
     wave_out.middle()
-    attend(docs_in, ctx_one, 0)
+    project(3, 6)
+    attend(docs_in, ctx_one, 0, 2, 4)
     wave_out.late()
 
     def block_member(i, pair=False):
@@ -526,16 +501,27 @@
     def columns_of(m):
         return pl.ds(pl.multiple_of(m * 256 + tensor * 128, 128), 128)
 
-    def summed(ctx, a, weights_of, up):
+    def summed(ctx, r, weights_of, up_of):
         total = None
+        rows = slice(r * 256, r * 256 + 256)
         for block in both:
             main = jnp.dot(
-                ctx[a * 256 : a * 256 + 256, block * 1024 : block * 1024 + 1024],
+                ctx[rows, block * 1024 : block * 1024 + 1024],
                 weights_of(block),
                 preferred_element_type=F32,
             )
-            value = main + jnp.dot(low[a, block], up, preferred_element_type=F32)
-            value = value.astype(BF16).astype(F32)
+            extra = jnp.concatenate(
+                [
+                    jnp.dot(
+                        low[block, (2 * r + a) * SEQ : (2 * r + a + 1) * SEQ],
+                        up_of(a),
+                        preferred_element_type=F32,
+                    )
+                    for a in both
+                ],
+                axis=0,
+            )
+            value = (main + extra).astype(BF16).astype(F32)
             total = value if total is None else total + value
         return total
 
@@ -550,27 +536,29 @@
         steps += [(i, 0), (i, 1)]
 
     def own_ref(n):
-        i, a = steps[n]
-        return h_next.at[block_member(i) * 2 + tensor, a]
+        i, r = steps[n]
+        return h_next.at[block_member(i) * 2 + tensor, r]
 
     def hop_copy(n):
         return block_copy(h_send.at[n], own_ref(n), 3, n, {"section": after})
 
     def start_block(n):
-        i, a = steps[n]
+        i, r = steps[n]
         f, dy = BLOCKS[i]
         slot = place.row(dy) * 2 + place.column(f) // 2
         columns = columns_of(block_member(i))
         total = summed(
-            ctx_one, a, lambda block: wo[slot, block * 1024 : block * 1024 + 1024],
-            up_all[a, :, columns],
+            ctx_one, r, lambda block: wo[slot, block * 1024 : block * 1024 + 1024],
+            lambda a: up_all[a, :, columns],
         )
-        h_send[n] = (h_all[a, :, columns].astype(F32) + total).astype(BF16)
+        for a in both:
+            rows = slice(a * SEQ, a * SEQ + SEQ)
+            h_send[n, rows] = (h_all[r, a, :, columns].astype(F32) + total[rows]).astype(BF16)
         hop_copy(n).start()
 
     def pair_ref(n):
-        i, a = steps[n]
-        return h_next.at[block_member(i, True) * 2 + tensor, a]
+        i, r = steps[n]
+        return h_next.at[block_member(i, True) * 2 + tensor, r]
 
     def pass_own(n, device, kind_of):
         return block_copy(own_ref(n), own_ref(n), kind_of, n, device)
@@ -588,16 +576,16 @@
         pass_pair(n).start()
 
     def other_ref(n, pair):
-        i, a = steps[n]
-        return h_next.at[block_member(i, pair) * 2 + other, a]
+        i, r = steps[n]
+        return h_next.at[block_member(i, pair) * 2 + other, r]
 
     def run(lower, upper):
         for n in range(lower, upper):
             start_block(n)
-            if n >= 2:
-                arrive(n - 2)
-            if n >= 5:
-                relay(n - 5)
+            if n >= 3:
+                arrive(n - 3)
+            if n >= 6:
+                relay(n - 6)
 
     collect(ctx_one, 0, 0)
     wave_out.end(0)
@@ -610,9 +598,9 @@
     run(12, 14)
     wave_out.end(3)
     run(14, 16)
-    for n in (14, 15):
+    for n in range(13, 16):
         arrive(n)
-    for n in range(11, 16):
+    for n in range(10, 16):
         relay(n)
     for n in range(16):
         ref = other_ref(n, False)
@@ -621,172 +609,185 @@
         block_copy(ref, ref, 2, n, to_other).wait_recv()
 
     def norm_second(i, carry):
-        a = i // 8
-        rows = pl.ds(pl.multiple_of(lax.rem(i, 8) * 32, 32), 32)
+        r, j = i // 8, lax.rem(i, 8)
+        a = j // 4
+        rows = pl.ds(pl.multiple_of(j * 32, 32), 32)
         total = jnp.zeros((32, 128), F32)
         for block in range(32):
-            h = h_next[block, a, rows, :].astype(F32)
+            h = h_next[block, r, rows, :].astype(F32)
             total = total + h * h
         scale = lax.rsqrt(jnp.sum(total, axis=-1, keepdims=True) * (1.0 / WIDTH) + EPS)
         scale = jnp.broadcast_to(scale, (32, 128))
         for block in range(32):
             columns = slice(block * 128, block * 128 + 128)
-            h = h_next[block, a, rows, :].astype(F32)
+            h = h_next[block, r, rows, :].astype(F32)
             nrm[pl.ds(pl.multiple_of(i * 32, 32), 32), columns] = (
                 h * scale * gain_all[a, :, columns]
             ).astype(BF16)
         return carry
 
-    lax.fori_loop(0, 16, norm_second, 0)
-    project()
-    attend(docs_next, ctx_two, 1)
+    for r in both:
+        lax.fori_loop(8 * r, 8 * r + 8, norm_second, 0)
+        project(3 * r, 3 * r + 3)
+        attend(docs_next, ctx_two, 1, 2 * r, 2 * r + 2)
 
     def pair_members(y):
         return y * SIDE + kind, y * SIDE + 3 - kind
 
-    def pair_columns(ref, a, y, half):
-        parts = []
-        for m in pair_members(y):
-            lower = (m - half * 8) * 256 + tensor * 128
-            parts.append(ref[a, :, pl.ds(pl.multiple_of(lower, 128), 128)])
-        return jnp.concatenate(parts, axis=1)
-
-    for a in both:
-        collect(ctx_two, 1, a)
-        square[a] = jnp.zeros((ROWS, 128), F32)
+    def up_pair(a, y):
+        return jnp.concatenate([up_all[a, :, columns_of(m)] for m in pair_members(y)], axis=1)
+
+    def last_output(r):
+        square[r] = jnp.zeros((ROWS, 128), F32)
 
         def last_block(y, carry):
             total = summed(
                 ctx_two,
-                a,
+                r,
                 lambda block: jnp.concatenate(
                     [wo[2 * y + k, block * 1024 : block * 1024 + 1024] for k in both], axis=1
                 ),
-                pair_columns(up_all, a, y, 0),
+                lambda a: up_pair(a, y),
             )
             for k, m in enumerate(pair_members(y)):
                 columns = slice(k * 128, k * 128 + 128)
-                h = h_next[m * 2 + tensor, a].astype(F32) + total[:, columns]
+                h = h_next[m * 2 + tensor, r].astype(F32) + total[:, columns]
                 h = h.astype(BF16)
-                h_last[a, y, :, columns] = h
+                h_last[r, y, :, columns] = h
                 h = h.astype(F32)
-                square[a] += h * h
+                square[r] += h * h
             return carry
 
         lax.fori_loop(0, SIDE, last_block, 0)
 
-    stat_own[...] = jnp.zeros_like(stat_own)
-    for a in both:
-        for r in both:
-            stat_own[2 * a + r : 2 * a + r + 1, :] = jnp.sum(
-                square[a, r * 128 : r * 128 + 128].T, axis=0, keepdims=True
+    def send_stats(r):
+        stat_own[r] = jnp.zeros((8, 128), F32)
+        for a in both:
+            stat_own[r, a : a + 1, :] = jnp.sum(
+                square[r, a * SEQ : a * SEQ + SEQ].T, axis=0, keepdims=True
             )
-    stats = [
-        misc(stat_own, stat_in.at[k], 13 + k, device)
-        for k, device in enumerate((to_other, to_pair, to_pair_other))
-    ]
-    for copy in stats:
-        copy.start()
-    for copy in stats:
-        copy.wait_recv()
-    total = stat_own[...] + stat_in[0] + stat_in[1] + stat_in[2]
-    scales = lax.rsqrt(total * (1.0 / WIDTH) + EPS)
-    column_scale = [jnp.broadcast_to(scales[s : s + 1], (128, 128)).T for s in range(4)]
-    for y in range(SIDE):
-        for k, m in enumerate((y * SIDE + kind, y * SIDE + 3 - kind)):
-            lower = (m - (y // 2) * 8) * 256 + tensor * 128
-            gains = [
-                final_all[a, y // 2, :, pl.ds(pl.multiple_of(lower, 128), 128)] for a in both
-            ]
-            columns = slice(k * 128, k * 128 + 128)
-            for r in both:
-                rows = slice(r * 128, r * 128 + 128)
+        stats = [
+            misc(stat_own.at[r], stat_in.at[r, k], 13 + 3 * r + k, device)
+            for k, device in enumerate((to_other, to_pair, to_pair_other))
+        ]
+        for copy in stats:
+            copy.start()
+        return stats
+
+    def rows_at(r, i):
+        return rows_out.at[r, pl.ds(pl.multiple_of(i * 16, 16), 16)]
+
+    def scatter_rows(r, stats):
+        for copy in stats:
+            copy.wait_recv()
+        total = stat_own[r] + stat_in[r, 0] + stat_in[r, 1] + stat_in[r, 2]
+        scales = lax.rsqrt(total * (1.0 / WIDTH) + EPS)
+        column_scale = [jnp.broadcast_to(scales[a : a + 1], (128, 128)).T for a in both]
+        for y in range(SIDE):
+            for k, m in enumerate(pair_members(y)):
+                lower = (m - (y // 2) * 8) * 256 + tensor * 128
+                gains = [
+                    final_all[a, y // 2, :, pl.ds(pl.multiple_of(lower, 128), 128)] for a in both
+                ]
+                columns = slice(k * 128, k * 128 + 128)
                 value = sum(
-                    h_last[a, y, rows, columns].astype(F32) * column_scale[2 * a + r] * gains[a]
+                    h_last[r, y, a * SEQ : a * SEQ + SEQ, columns].astype(F32)
+                    * column_scale[a]
+                    * gains[a]
                     for a in both
                 )
-                rows_out[rows, (2 * y + k) * 128 : (2 * y + k + 1) * 128] = value.astype(BF16)
-
-    def rows_at(i):
-        return rows_out.at[pl.ds(pl.multiple_of(i * 32, 32), 32)]
-
-    def scatter(i, carry):
-        f, dy = lax.rem(i, 2), i // 2
-        x, y = place.column(f), place.row(dy)
-        pltpu.make_async_remote_copy(
-            rows_at(y * 2 + x // 2), rows_in.at[index8], scatter_s, scatter_r,
-            {"member": y * SIDE + x}, MESH,
+                rows_out[r, :, (2 * y + k) * 128 : (2 * y + k + 1) * 128] = value.astype(BF16)
+
+        def scatter(i, carry):
+            f, dy = lax.rem(i, 2), i // 2
+            x, y = place.column(f), place.row(dy)
+            pltpu.make_async_remote_copy(
+                rows_at(r, y * 2 + x // 2), rows_in.at[r, index8], scatter_s.at[r], scatter_r.at[r],
+                {"member": y * SIDE + x}, MESH,
+            ).start()
+            return carry
+
+        lax.fori_loop(1, 8, scatter, 0)
+        return local(rows_at(r, index8), rows_in.at[r, index8], 7 + r)
+
+    def seven(r):
+        ref = rows_in.at[r, pl.ds(0, 7)]
+        return pltpu.make_async_remote_copy(
+            ref, ref, scatter_s.at[r], scatter_r.at[r], to_other, MESH
+        )
+
+    def average(r, keep):
+        keep.wait()
+        seven(r).wait_recv()
+        total = rows_in[r, 0].astype(F32)
+        for i in range(1, 8):
+            total = total + rows_in[r, i].astype(F32)
+        total = (total * (1.0 / MEMBERS)).astype(BF16)
+        for half in both:
+            mean_own[r, half] = total[:, half * 512 : half * 512 + 512]
+        misc(mean_own.at[r, tensor], mean_in.at[r, tensor], 19 + 2 * r, {"section": after}).start()
+        misc(
+            mean_own.at[r, other], mean_in.at[r, tensor], 20 + 2 * r,
+            {"section": after, "tensor": other},
         ).start()
-        return carry
-
-    lax.fori_loop(1, 8, scatter, 0)
-    keep = local(rows_at(index8), rows_in.at[index8], 7)
-    keep.wait()
-    seven = pltpu.make_async_remote_copy(
-        rows_in.at[pl.ds(0, 7)], rows_in.at[pl.ds(0, 7)], scatter_s, scatter_r, to_other, MESH
-    )
-    seven.wait_recv()
-    total = rows_in[0].astype(F32)
-    for i in range(1, 8):
-        total = total + rows_in[i].astype(F32)
-    total = (total * (1.0 / MEMBERS)).astype(BF16)
-    for half in both:
-        mean_own[half] = total[:, half * 512 : half * 512 + 512]
-    hops = [
-        misc(mean_own.at[tensor], mean_in.at[tensor], 16, {"section": after}),
-        misc(mean_own.at[other], mean_in.at[tensor], 17, {"section": after, "tensor": other}),
-    ]
-    for copy in hops:
-        copy.start()
-    hops[0].wait_recv()
-    pltpu.make_async_remote_copy(
-        mean_own.at[other], mean_in.at[other], misc_s.at[17], misc_r.at[17],
-        {"section": after, "tensor": other}, MESH,
-    ).wait_recv()
-
-    def mean_slot(part, slot, which):
-        if which is None:
-            return fin.at[slot, part]
-        return fin.at[slot, part, :, pl.ds(which * 256, 256)]
-
-    final = Gather(
-        place,
-        lambda part: mean_in.at[part],
-        mean_slot,
-        lambda part: fin.at[pl.ds(0, 15), part],
-        ag_send,
-        ag_recv,
-    )
-    for part in both:
-        final.first(part)
-    for part in both:
-        final.spread(part, 0)
-    fin[member] = mean_in[...]
-    for part in both:
-        final.line(part)
-    for part in both:
-        final.cross(part, 0)
-    for part in both:
-        final.far(part)
-    for q in (1, 2, 3):
-        for part in both:
-            final.cross(part, q)
-    for q in range(SIDE):
-        for part in both:
-            final.last(part, q)
-    for m in range(MEMBERS):
-        x, y = m % SIDE, m // SIDE
-        side = ((x + 1) // 2) % 2
-        rows = slice((y * 2 + x // 2) * 32, (y * 2 + x // 2) * 32 + 32)
-        for part in both:
-            for s in range(4):
-                column = (s // 2 * SIDE + (side if s % 2 == 0 else 3 - side)) * 256 + part * 128
-                out_ref[rows, column : column + 128] = fin[m, part, :, s * 128 : s * 128 + 128]
+
+    def hopped(r):
+        for half, index in ((tensor, 19 + 2 * r), (other, 20 + 2 * r)):
+            ref = mean_in.at[r, half]
+            pltpu.make_async_remote_copy(
+                ref, ref, misc_s.at[index], misc_r.at[index], to_other, MESH
+            ).wait_recv()
+
+    def gather_of(r):
+        return PlaneGather(
+            place,
+            lambda part: mean_in.at[r, part],
+            lambda part, slot: fin.at[r, slot, part],
+            lambda part: fin.at[r, pl.ds(0, 15), part],
+            ag_send.at[r],
+            ag_recv.at[r],
+        )
+
+    collect(ctx_two, 1, 0)
+    last_output(0)
+    keep_zero = scatter_rows(0, send_stats(0))
+    collect(ctx_two, 1, 1)
+    last_output(1)
+    stats_one = send_stats(1)
+    average(0, keep_zero)
+    keep_one = scatter_rows(1, stats_one)
+    final_zero, final_one = gather_of(0), gather_of(1)
+    hopped(0)
+    final_zero.begin()
+    fin[0, member] = mean_in[0]
+    average(1, keep_one)
+    final_zero.middle()
+    hopped(1)
+    final_one.begin()
+    fin[1, member] = mean_in[1]
+    final_zero.end()
+
+    def place_rows(r):
+        for m in range(MEMBERS):
+            x, y = m % SIDE, m // SIDE
+            side = ((x + 1) // 2) % 2
+            lower = r * SEQ + (y * 2 + x // 2) * 16
+            for part in both:
+                for s in range(4):
+                    column = (s // 2 * SIDE + (side if s % 2 == 0 else 3 - side)) * 256 + part * 128
+                    out_ref[lower : lower + 16, column : column + 128] = fin[
+                        r, m, part, :, s * 128 : s * 128 + 128
+                    ]
+
+    final_one.middle()
+    place_rows(0)
+    final_one.end()
+    place_rows(1)
 
     for wave in (wave_one, wave_two, wave_out):
         wave.sent()
-    for part in both:
-        final.sent(part)
+    final_zero.sent()
+    final_one.sent()
     for tick, ctx in enumerate((ctx_one, ctx_two)):
         for which in range(3):
             for s in range(4):
@@ -798,7 +799,8 @@
         pass_pair(n).wait_send()
     for copy in pending:
         copy.wait_send()
-    seven.wait_send()
+    for r in both:
+        seven(r).wait_send()
 
 
 def per_device(
@@ -823,12 +825,12 @@
         scratch_shapes=[
             pltpu.VMEM((WIDTH, 768), BF16),
             pltpu.VMEM((8, 2048, 128), BF16),
-            pltpu.VMEM((2, ROWS, WIDTH), BF16),
+            pltpu.VMEM((2, 2, SEQ, WIDTH), BF16),
             pltpu.VMEM((2 * ROWS, WIDTH), BF16),
             pltpu.VMEM((2 * ROWS, 768), F32),
             pltpu.VMEM((2 * ROWS, 2048), BF16),
             pltpu.VMEM((2 * ROWS, 2048), BF16),
-            pltpu.VMEM((2, 2, ROWS, 16), BF16),
+            pltpu.VMEM((2, 2 * ROWS, 16), BF16),
             pltpu.VMEM((2, SEQ), jnp.int32),
             pltpu.VMEM((2, 1, WIDTH), F32),
             pltpu.VMEM((2, 2, 16, 1024), BF16),
@@ -838,35 +840,35 @@
             pltpu.VMEM((32, 2, ROWS, 128), BF16),
             pltpu.VMEM((2, SIDE, ROWS, 256), BF16),
             pltpu.VMEM((2, ROWS, 128), F32),
-            pltpu.VMEM((8, 128), F32),
-            pltpu.VMEM((3, 8, 128), F32),
-            pltpu.VMEM((ROWS, 1024), BF16),
-            pltpu.VMEM((8, 32, 1024), BF16),
-            pltpu.VMEM((2, 32, 512), BF16),
-            pltpu.VMEM((2, 32, 512), BF16),
-            pltpu.VMEM((MEMBERS, 2, 32, 512), BF16),
+            pltpu.VMEM((2, 8, 128), F32),
+            pltpu.VMEM((2, 3, 8, 128), F32),
+            pltpu.VMEM((2, SEQ, 1024), BF16),
+            pltpu.VMEM((2, 8, 16, 1024), BF16),
+            pltpu.VMEM((2, 2, 16, 512), BF16),
+            pltpu.VMEM((2, 2, 16, 512), BF16),
+            pltpu.VMEM((2, MEMBERS, 2, 16, 512), BF16),
             dma((3, 2)),
             dma((3, 2, 7)),
-            dma((2,)),
-            dma((2, 15)),
-            dma((8,)),
+            dma((2, 2)),
+            dma((2, 2, 15)),
+            dma((9,)),
             dma((2, 3, 4)),
             dma((2, 3, 4)),
             dma((16,)),
             dma((16,)),
             dma((3, 16)),
             dma((3, 16)),
-            dma((18,)),
-            dma((18,)),
-            dma,
-            dma,
+            dma((23,)),
+            dma((23,)),
+            dma((2,)),
+            dma((2,)),
         ],
         compiler_params=pltpu.CompilerParams(
             collective_id=0, has_side_effects=True, vmem_limit_bytes=58 * 1024 * 1024
         ),
         name="relay",
     )(
-        hidden_input.reshape(ROWS, WIDTH),
+        hidden_input.reshape(2, SEQ, WIDTH),
         document_index[0],
         query_key_value_weight[0].reshape(256, 1536),
         output_weight[0],

time: 178 us -> 163 us (0.916)
  Pallas kernels: 172 us -> 159 us
    pallas_call x1, Pallas kernels: 172 us -> 159 us  [per_device(): pl.pallas_call(kernel, out_shape=jax.ShapeDtypeStruct((ROWS, WIDTH // 2),...]
where the time goes in v3:
time: 163 us
  Pallas kernels  159 us (98%)
  local copies, waits for them, and re-layouts  4.4 us (3%)
    pallas_call x1, Pallas kernels, per_device(): pl.pallas_call(kernel, out_shape=jax.ShapeDtypeStruct((ROWS, WIDTH // 2),...  159 us
    unnamed x2, local copies, waits for them, and re-layouts  4.4 us

profile of v3, /device:TPU:1, one launch (start us, length us, event | category | flops | bytes accessed | tf_op | source)
XLA Modules:
  0.0 163.0 jit_solution(6472150339572886784)
XLA Ops:
  0.0 2.1 %copy.11 = bf16[32,8,2,768]{3,1,2,0:T(8,128)(2,1)} copy(bf16[32,8,2,768]{3,2,1,0:T(2,128)(2,1)} %bitcast.15) | data formatting | bytes 1572864
  2.1 158.5 %relay.1 = bf16[256,2048]{1,0:T(8,128)(2,1)} custom-call(bf16[2,128,4096]{2,1,0:T(8,128)(2,1)} %bitcast.14, s32[2,128]{1,0:T(2,128)} %bitcast.20, bf16[256,1536]{1,0:T(8,128)(2,1)} %bitcast.13, bf16[1024,256]{1,0:T(8,128)(2,1)} %bitcast.16, bf16[16,1024]{1,0:T(8,128)(2,1)} %bitcast.18, bf16[16,4096]{1,0:T(8,128)(2,1)} %bitcast.17, f32[1,4096]{1,0:T(1,128)} %bitcast.19, ...), custom_call_target="tpu_custom_call" | custom-call | tf_op jit(solution)/shard_map/relay/pallas_call | solution.py:820
  160.6 2.3 %copy.13 = bf16[1,2,128,2048]{3,2,1,0:T(8,128)(2,1)} copy(bf16[1,2,128,2048]{3,2,1,0:T(8,128)(2,1)} %bitcast.12) | data formatting | bytes 2097152

commit v4 on v3

--- a/solution.py
+++ b/solution.py
@@ -103,10 +103,12 @@
             for index, (f, dy) in enumerate(targets):
                 self.copy(self.own(part), self.ref(part, 0, 0), part, f, dy, index).start()
 
-    def middle(self):
+    def cross_near(self):
         self.wait(0, 1, 0, 0)
         self.move(0, 1, 0, None, 0, 1, 3)
         self.move(0, 1, 0, None, 0, -1, 4)
+
+    def round_near(self):
         self.wait(1, 0, -1, 0)
         self.move(1, 0, -1, 0, 0, 1, 3)
         self.move(1, 0, -1, None, 1, 0, 4)
@@ -114,17 +116,30 @@
         self.move(1, 0, 1, 1, 0, -1, 3)
         self.move(1, 0, 1, None, 1, 0, 5)
 
-    def late(self):
+    def own_far(self):
         self.wait(0, 0, -1, 1)
         self.move(0, 0, -1, 0, 0, 1, 5)
         self.wait(0, 0, 1, 2)
         self.move(0, 0, 1, 1, 0, -1, 5)
+
+    def round_far(self):
         self.wait(1, 0, 2, 3)
         self.move(1, 0, 2, None, 1, 0, 6)
+
+    def cross_far(self):
         self.wait(0, 1, -1, 3)
         self.move(0, 1, -1, 0, 0, 1, 6)
         self.wait(0, 1, 1, 4)
         self.move(0, 1, 1, 1, 0, -1, 6)
+
+    def middle(self):
+        self.cross_near()
+        self.round_near()
+
+    def late(self):
+        self.own_far()
+        self.round_far()
+        self.cross_far()
 
     def end(self, stage):
         if stage == 0:
@@ -489,10 +504,11 @@
         wave_two.end(stage)
     project(0, 3)
     attend(docs_in, ctx_one, 0, 0, 2)
-    wave_out.middle()
     project(3, 6)
     attend(docs_in, ctx_one, 0, 2, 4)
-    wave_out.late()
+    wave_out.cross_near()
+    wave_out.own_far()
+    wave_out.round_near()
 
     def block_member(i, pair=False):
         f, dy = BLOCKS[i]
@@ -531,9 +547,7 @@
         )
         return pltpu.make_async_remote_copy(ref, dst, send, recv, device, MESH)
 
-    steps = [(i, 0) for i in range(4)] + [(i, 1) for i in range(4)]
-    for i in range(4, 8):
-        steps += [(i, 0), (i, 1)]
+    steps = [(i, r) for lower in (0, 4) for r in both for i in range(lower, lower + 4)]
 
     def own_ref(n):
         i, r = steps[n]
@@ -582,31 +596,34 @@
     def run(lower, upper):
         for n in range(lower, upper):
             start_block(n)
-            if n >= 3:
-                arrive(n - 3)
-            if n >= 6:
-                relay(n - 6)
+            if n >= 4:
+                arrive(n - 4)
+            if n >= 7:
+                relay(n - 7)
 
     collect(ctx_one, 0, 0)
     wave_out.end(0)
     run(0, 4)
+    wave_out.cross_far()
     collect(ctx_one, 0, 1)
+    wave_out.round_far()
     run(4, 8)
     wave_out.end(1)
-    run(8, 12)
+    run(8, 10)
     wave_out.end(2)
-    run(12, 14)
+    run(10, 11)
     wave_out.end(3)
-    run(14, 16)
-    for n in range(13, 16):
-        arrive(n)
-    for n in range(10, 16):
+    run(11, 16)
+    for n in (9, 10, 11):
         relay(n)
-    for n in range(16):
-        ref = other_ref(n, False)
-        block_copy(ref, ref, 1, n, to_other).wait_recv()
-        ref = other_ref(n, True)
-        block_copy(ref, ref, 2, n, to_other).wait_recv()
+
+    def complete(r):
+        for n in range(16):
+            if steps[n][1] == r:
+                ref = other_ref(n, False)
+                block_copy(ref, ref, 1, n, to_other).wait_recv()
+                ref = other_ref(n, True)
+                block_copy(ref, ref, 2, n, to_other).wait_recv()
 
     def norm_second(i, carry):
         r, j = i // 8, lax.rem(i, 8)
@@ -626,10 +643,22 @@
             ).astype(BF16)
         return carry
 
-    for r in both:
-        lax.fori_loop(8 * r, 8 * r + 8, norm_second, 0)
-        project(3 * r, 3 * r + 3)
-        attend(docs_next, ctx_two, 1, 2 * r, 2 * r + 2)
+    complete(0)
+    arrive(12)
+    lax.fori_loop(0, 8, norm_second, 0)
+    arrive(13)
+    relay(12)
+    project(0, 3)
+    arrive(14)
+    arrive(15)
+    relay(13)
+    attend(docs_next, ctx_two, 1, 0, 2)
+    relay(14)
+    relay(15)
+    complete(1)
+    lax.fori_loop(8, 16, norm_second, 0)
+    project(3, 6)
+    attend(docs_next, ctx_two, 1, 2, 4)
 
     def pair_members(y):
         return y * SIDE + kind, y * SIDE + 3 - kind

time: 163 us -> 157 us (0.963)
  Pallas kernels: 159 us -> 152 us
    pallas_call x1, Pallas kernels: 159 us -> 152 us  [per_device(): pl.pallas_call(kernel, out_shape=jax.ShapeDtypeStruct((ROWS, WIDTH // 2),...]
where the time goes in v4:
time: 157 us
  Pallas kernels  152 us (97%)
  local copies, waits for them, and re-layouts  4.4 us (3%)
    pallas_call x1, Pallas kernels, per_device(): pl.pallas_call(kernel, out_shape=jax.ShapeDtypeStruct((ROWS, WIDTH // 2),...  152 us
    unnamed x2, local copies, waits for them, and re-layouts  4.4 us

profile of v4, /device:TPU:1, one launch (start us, length us, event | category | flops | bytes accessed | tf_op | source)
XLA Modules:
  0.0 156.8 jit_solution(15538528395284179032)
XLA Ops:
  0.0 2.1 %copy.11 = bf16[32,8,2,768]{3,1,2,0:T(8,128)(2,1)} copy(bf16[32,8,2,768]{3,2,1,0:T(2,128)(2,1)} %bitcast.15) | data formatting | bytes 1572864
  2.1 152.4 %relay.1 = bf16[256,2048]{1,0:T(8,128)(2,1)} custom-call(bf16[2,128,4096]{2,1,0:T(8,128)(2,1)} %bitcast.14, s32[2,128]{1,0:T(2,128)} %bitcast.20, bf16[256,1536]{1,0:T(8,128)(2,1)} %bitcast.13, bf16[1024,256]{1,0:T(8,128)(2,1)} %bitcast.16, bf16[16,1024]{1,0:T(8,128)(2,1)} %bitcast.18, bf16[16,4096]{1,0:T(8,128)(2,1)} %bitcast.17, f32[1,4096]{1,0:T(1,128)} %bitcast.19, ...), custom_call_target="tpu_custom_call" | custom-call | tf_op jit(solution)/shard_map/relay/pallas_call | solution.py:849
  154.5 2.3 %copy.13 = bf16[1,2,128,2048]{3,2,1,0:T(8,128)(2,1)} copy(bf16[1,2,128,2048]{3,2,1,0:T(8,128)(2,1)} %bitcast.12) | data formatting | bytes 2097152

commit v5 on v4

--- a/solution.py
+++ b/solution.py
@@ -232,7 +232,7 @@
 def kernel(
     hidden_in, docs_in, qkv_in, out_in, down_in, up_in, gain_in, final_in, cos_ref, sin_ref,
     out_ref,
-    wq, wo, h_all, nrm, proj, ctx_one, ctx_two, low, docs_next, gain_all, down_all, up_all, final_all,
+    wq, wo, h_all, nrm, proj, ctx_one, ctx_two, held, low, docs_next, gain_all, down_all, up_all, final_all,
     h_send, h_next, h_last, square, stat_own, stat_in, rows_out, rows_in, mean_own, mean_in, fin,
     pg_send, pg_recv, ag_send, ag_recv, local_sem, ctx_s, ctx_r, hop_s, hop_r, fwd_s, fwd_r,
     misc_s, misc_r, scatter_s, scatter_r,
@@ -296,21 +296,31 @@
     )
     pl.semaphore_wait(barrier, MEMBERS - 1 + 6)
 
-    def qkv_slot(of_pair):
+    COLUMNS = ((0, 512), (512, 256))
+
+    def group_columns(group, base=0):
+        lower, size = COLUMNS[group]
+        return pl.ds(pl.multiple_of(base + lower, 256), size)
+
+    def qkv_wave(group, of_pair):
         def slot(x, y, part, which):
             if of_pair:
                 x = x + 1 - 2 * lax.rem(x, 2)
             lower, size = cut(QKV_SPLIT, part, which)
-            return wq.at[pl.ds(pl.multiple_of((y * SIDE + x) * 256 + lower, 16), size)]
-
-        return slot
-
-    def own_qkv(part):
-        lower, size = cut(QKV_SPLIT, part, None)
-        return qkv_in.at[pl.ds(lower, size), pl.ds(pl.multiple_of(kind * 768, 256), 768)]
-
-    def whole_qkv(part):
-        return wq.at[pl.ds(0, 7 * cut(QKV_SPLIT, part, None)[1])]
+            rows = pl.ds(pl.multiple_of((y * SIDE + x) * 256 + lower, 16), size)
+            return wq.at[rows, group_columns(group)]
+
+        def own(part):
+            lower, size = cut(QKV_SPLIT, part, None)
+            if of_pair:
+                return slot(place.x, place.y, part, None)
+            return qkv_in.at[pl.ds(lower, size), group_columns(group, kind * 768)]
+
+        def whole(part):
+            return wq.at[pl.ds(0, 7 * cut(QKV_SPLIT, part, None)[1]), group_columns(group)]
+
+        n = 2 * group + of_pair
+        return PairGather(place, own, slot, whole, pg_send.at[n], pg_recv.at[n])
 
     def out_slot(x, y, part, which):
         lower, size = cut(OUT_SPLIT, part, which)
@@ -319,35 +329,38 @@
     def whole_out(part):
         return wo.at[pl.ds(0, 7), pl.ds(0, cut(OUT_SPLIT, part, None)[1])]
 
-    wave_one = PairGather(place, own_qkv, qkv_slot(False), whole_qkv, pg_send.at[0], pg_recv.at[0])
-    pair_slot = qkv_slot(True)
-    wave_two = PairGather(
-        place,
-        lambda part: pair_slot(place.x, place.y, part, None),
-        pair_slot,
-        whole_qkv,
-        pg_send.at[1],
-        pg_recv.at[1],
-    )
+    waves = [qkv_wave(group, of_pair) for group in both for of_pair in both]
     wave_out = PairGather(
         place,
         lambda part: out_slot(place.x, place.y, part, None),
         out_slot,
         whole_out,
-        pg_send.at[2],
-        pg_recv.at[2],
+        pg_send.at[4],
+        pg_recv.at[4],
     )
 
     to_pair = {"member": place.pair}
     to_pair_other = {"member": place.pair, "tensor": other}
     to_other = {"tensor": other}
 
-    rows_of = lambda m: wq.at[pl.ds(pl.multiple_of(m * 256, 256), 256)]
-    seed = misc(
-        qkv_in.at[:, pl.ds(pl.multiple_of((1 - kind) * 768, 256), 768)], rows_of(member), 0, to_pair
-    )
-    seed.start()
-    wave_one.begin()
+    def seed_rows(m, group):
+        return wq.at[pl.ds(pl.multiple_of(m * 256, 256), 256), group_columns(group)]
+
+    def seed_copy(group):
+        return misc(
+            qkv_in.at[:, group_columns(group, (1 - kind) * 768)], seed_rows(member, group),
+            0 if group == 0 else 23, to_pair,
+        )
+
+    def seeded(group):
+        ref, index = seed_rows(place.pair, group), 0 if group == 0 else 23
+        pltpu.make_async_remote_copy(
+            ref, ref, misc_s.at[index], misc_r.at[index], to_pair, MESH
+        ).wait_recv()
+
+    seed_copy(0).start()
+    waves[0].begin()
+    seed_copy(1).start()
     half_of = lambda a, t: h_all.at[t, a]
     share_h = misc(
         hidden_in.at[tensor], half_of(parity, tensor), 1, to_pair
@@ -384,80 +397,86 @@
 
     norm_first(parity)
 
-    def project(lower, upper):
+    def project(r, group):
+        rows = slice(r * 256, r * 256 + 256)
+
         def block(n, carry):
-            rows = pl.ds(pl.multiple_of(n // 3 * 256, 256), 256)
-            columns = pl.ds(pl.multiple_of(lax.rem(n, 3) * 256, 256), 256)
+            columns = pl.ds(pl.multiple_of(n * 256, 256), 256)
             proj[rows, columns] = jnp.dot(nrm[rows, :], wq[:, columns], preferred_element_type=F32)
             return carry
 
-        lax.fori_loop(lower, upper, block, 0)
+        lax.fori_loop(2 * group, 2 + group, block, 0)
 
     ahead = lax.broadcasted_iota(jnp.int32, (SEQ, SEQ), 0) >= lax.broadcasted_iota(
         jnp.int32, (SEQ, SEQ), 1
     )
     head = 2 * tensor + kind
 
-    def ctx_copy(ctx, tick, s, which):
-        owner = 2 * tensor + (1 - kind if which == 2 else kind)
-        ref = ctx.at[
-            pl.ds(pl.multiple_of(s * SEQ, SEQ), SEQ), pl.ds(pl.multiple_of(owner * 512, 512), 512)
+    def ctx_part(ctx, s, group, owner):
+        return ctx.at[
+            pl.ds(pl.multiple_of(s * SEQ, SEQ), SEQ),
+            pl.ds(pl.multiple_of(owner * 512 + group * 256, 256), 256),
         ]
+
+    def ctx_copy(ctx, tick, s, group, which):
+        ref = ctx_part(ctx, s, group, 2 * tensor + (1 - kind if which == 2 else kind))
+        n = 2 * s + group
         return pltpu.make_async_remote_copy(
-            ref, ref, ctx_s.at[tick, which, s], ctx_r.at[tick, which, s],
+            ref, ref, ctx_s.at[tick, which, n], ctx_r.at[tick, which, n],
             to_pair if which == 1 else to_other, MESH,
         )
 
-    def ctx_arrived(ctx, tick, s, which):
+    def ctx_arrived(ctx, tick, s, group, which):
         t = tensor if which == 1 else other
-        owner = 2 * t + (kind if which == 0 else 1 - kind)
-        ref = ctx.at[
-            pl.ds(pl.multiple_of(s * SEQ, SEQ), SEQ), pl.ds(pl.multiple_of(owner * 512, 512), 512)
-        ]
+        ref = ctx_part(ctx, s, group, 2 * t + (kind if which == 0 else 1 - kind))
+        n = 2 * s + group
         pltpu.make_async_remote_copy(
-            ref, ref, ctx_s.at[tick, which, s], ctx_r.at[tick, which, s], to_other, MESH
+            ref, ref, ctx_s.at[tick, which, n], ctx_r.at[tick, which, n], to_other, MESH
         ).wait_recv()
 
-    def attend(docs_ref, ctx, tick, lower, upper):
+    def attend(docs_ref, ctx, tick, r, group):
         def sequence(s, carry):
             rows = pl.ds(pl.multiple_of(s * SEQ, SEQ), SEQ)
-            numbers = docs_ref[pl.ds(s // 2, 1), :]
-            numbers = jnp.broadcast_to(numbers, (SEQ, SEQ)).astype(F32)
+            numbers = jnp.broadcast_to(docs_ref[r : r + 1, :], (SEQ, SEQ)).astype(F32)
             allowed = ahead & (numbers == numbers.T)
-            allowed = jnp.concatenate([allowed.astype(F32)] * GROUP, axis=0) > 0.5
+            allowed = jnp.concatenate([allowed.astype(F32)] * 2, axis=0) > 0.5
             cosine, sine = cos_ref[...], sin_ref[...]
 
             def piece(g):
                 return proj[rows, g * 128 : g * 128 + 128]
 
+            if group == 0:
+                held[s, 0] = rotate(piece(0), cosine, sine)
+                held[s, 1] = piece(1).astype(BF16)
             queries = jnp.concatenate(
-                [rotate(piece(g), cosine, sine) for g in range(GROUP)], axis=0
+                [rotate(piece(2 + 2 * group + g), cosine, sine) for g in both], axis=0
             )
-            keys = rotate(piece(GROUP), cosine, sine)
-            values = piece(GROUP + 1).astype(BF16)
             scores = lax.dot_general(
-                queries, keys, (((1,), (1,)), ((), ())), preferred_element_type=F32
+                queries, held[s, 0], (((1,), (1,)), ((), ())), preferred_element_type=F32
             ) * (1.0 / math.sqrt(HEAD_WIDTH))
             scores = jnp.where(allowed, scores, -1e30)
             weights = jnp.exp(scores - jnp.max(scores, axis=-1, keepdims=True))
             weights = (weights / jnp.sum(weights, axis=-1, keepdims=True)).astype(BF16)
-            context = jnp.dot(weights, values, preferred_element_type=F32).astype(BF16)
-            for g in range(GROUP):
-                columns = pl.ds(pl.multiple_of(head * 512 + g * 128, 128), 128)
+            context = jnp.dot(weights, held[s, 1], preferred_element_type=F32).astype(BF16)
+            for g in both:
+                columns = pl.ds(pl.multiple_of(head * 512 + group * 256 + g * 128, 128), 128)
                 ctx[rows, columns] = context[g * SEQ : (g + 1) * SEQ]
-            ctx_copy(ctx, tick, s, 1).start()
-            ctx_copy(ctx, tick, s, 0).start()
+            ctx_copy(ctx, tick, s, group, 1).start()
+            ctx_copy(ctx, tick, s, group, 0).start()
             return carry
 
-        lax.fori_loop(lower, upper, sequence, 0)
+        lax.fori_loop(2 * r, 2 * r + 2, sequence, 0)
+
+    def relay_contexts(ctx, tick, r, group):
+        for a in both:
+            ctx_arrived(ctx, tick, 2 * r + a, group, 1)
+            ctx_copy(ctx, tick, 2 * r + a, group, 2).start()
 
     def collect(ctx, tick, r):
         for a in both:
-            ctx_arrived(ctx, tick, 2 * r + a, 1)
-            ctx_copy(ctx, tick, 2 * r + a, 2).start()
-        for a in both:
-            ctx_arrived(ctx, tick, 2 * r + a, 0)
-            ctx_arrived(ctx, tick, 2 * r + a, 2)
+            for group in both:
+                ctx_arrived(ctx, tick, 2 * r + a, group, 0)
+                ctx_arrived(ctx, tick, 2 * r + a, group, 2)
         for a in both:
             rows = slice((2 * r + a) * SEQ, (2 * r + a + 1) * SEQ)
             for block in both:
@@ -468,47 +487,60 @@
                     preferred_element_type=F32,
                 ).astype(BF16)
 
-    wave_one.middle()
-    seed_in = pltpu.make_async_remote_copy(
-        rows_of(place.pair), rows_of(place.pair), misc_s.at[0], misc_r.at[0], to_pair, MESH
-    )
-    seed_in.wait_recv()
-    wave_two.begin()
-    wave_one.late()
+    waves[0].middle()
+    seeded(0)
+    waves[1].begin()
+    waves[0].late()
     pltpu.make_async_remote_copy(
         half_of(1 - parity, tensor), half_of(1 - parity, tensor), misc_s.at[1], misc_r.at[1],
         to_pair, MESH,
     ).wait_recv()
     pass_h = misc(half_of(1 - parity, tensor), half_of(1 - parity, tensor), 12, to_other)
     pass_h.start()
-    wave_two.middle()
-    load_o.wait()
-    share_in = wo.at[index8, pl.ds(pl.multiple_of(other * 1024, 1024), 1024)]
-    pltpu.make_async_remote_copy(
-        share_in, share_in, misc_s.at[2], misc_r.at[2], to_other, MESH
-    ).wait_recv()
-    wave_two.late()
+    waves[1].middle()
+    waves[2].begin()
+    waves[1].late()
     pltpu.make_async_remote_copy(
         half_of(1 - parity, other), half_of(1 - parity, other), misc_s.at[12], misc_r.at[12],
         to_other, MESH,
     ).wait_recv()
     small[0].wait_recv()
     norm_first(1 - parity)
-    wave_out.begin()
+    load_o.wait()
+    share_in = wo.at[index8, pl.ds(pl.multiple_of(other * 1024, 1024), 1024)]
+    pltpu.make_async_remote_copy(
+        share_in, share_in, misc_s.at[2], misc_r.at[2], to_other, MESH
+    ).wait_recv()
     for copy in small[1:]:
         copy.wait_recv()
     for copy in loads[1:]:
         copy.wait()
+    seeded(1)
+    waves[2].middle()
+    waves[3].begin()
     for stage in range(4):
-        wave_one.end(stage)
-        wave_two.end(stage)
-    project(0, 3)
-    attend(docs_in, ctx_one, 0, 0, 2)
-    project(3, 6)
-    attend(docs_in, ctx_one, 0, 2, 4)
+        waves[0].end(stage)
+        waves[1].end(stage)
+    waves[2].late()
+    project(0, 0)
+    attend(docs_in, ctx_one, 0, 0, 0)
+    waves[3].middle()
+    project(1, 0)
+    attend(docs_in, ctx_one, 0, 1, 0)
+    waves[3].late()
+    wave_out.begin()
+    relay_contexts(ctx_one, 0, 0, 0)
+    for stage in range(4):
+        waves[2].end(stage)
+        waves[3].end(stage)
+    project(0, 1)
+    attend(docs_in, ctx_one, 0, 0, 1)
+    project(1, 1)
+    attend(docs_in, ctx_one, 0, 1, 1)
     wave_out.cross_near()
     wave_out.own_far()
-    wave_out.round_near()
+    relay_contexts(ctx_one, 0, 1, 0)
+    relay_contexts(ctx_one, 0, 0, 1)
 
     def block_member(i, pair=False):
         f, dy = BLOCKS[i]
@@ -547,7 +579,8 @@
         )
         return pltpu.make_async_remote_copy(ref, dst, send, recv, device, MESH)
 
-    steps = [(i, r) for lower in (0, 4) for r in both for i in range(lower, lower + 4)]
+    steps = [(i, r) for r in both for i in range(4)] + [(i, r) for r in both for i in (4, 5)]
+    steps += [(i, r) for i in (6, 7) for r in both]
 
     def own_ref(n):
         i, r = steps[n]
@@ -602,20 +635,27 @@
                 relay(n - 7)
 
     collect(ctx_one, 0, 0)
+    run(0, 1)
+    wave_out.round_near()
+    relay_contexts(ctx_one, 0, 1, 1)
     wave_out.end(0)
-    run(0, 4)
+    run(1, 4)
     wave_out.cross_far()
     collect(ctx_one, 0, 1)
+    run(4, 8)
     wave_out.round_far()
-    run(4, 8)
     wave_out.end(1)
-    run(8, 10)
+    run(8, 12)
     wave_out.end(2)
-    run(10, 11)
+    run(12, 14)
     wave_out.end(3)
-    run(11, 16)
-    for n in (9, 10, 11):
-        relay(n)
+    run(14, 16)
+    relay(9)
+    relay(10)
+    for n in range(12, 16):
+        arrive(n)
+        relay(n - 1)
+    relay(15)
 
     def complete(r):
         for n in range(16):
@@ -643,22 +683,12 @@
             ).astype(BF16)
         return carry
 
-    complete(0)
-    arrive(12)
-    lax.fori_loop(0, 8, norm_second, 0)
-    arrive(13)
-    relay(12)
-    project(0, 3)
-    arrive(14)
-    arrive(15)
-    relay(13)
-    attend(docs_next, ctx_two, 1, 0, 2)
-    relay(14)
-    relay(15)
-    complete(1)
-    lax.fori_loop(8, 16, norm_second, 0)
-    project(3, 6)
-    attend(docs_next, ctx_two, 1, 2, 4)
+    for r in both:
+        complete(r)
+        lax.fori_loop(8 * r, 8 * r + 8, norm_second, 0)
+        for group in both:
+            project(r, group)
+            attend(docs_next, ctx_two, 1, r, group)
 
     def pair_members(y):
         return y * SIDE + kind, y * SIDE + 3 - kind
@@ -777,20 +807,24 @@
             ag_recv.at[r],
         )
 
+    relay_contexts(ctx_two, 1, 0, 0)
+    relay_contexts(ctx_two, 1, 0, 1)
     collect(ctx_two, 1, 0)
     last_output(0)
     keep_zero = scatter_rows(0, send_stats(0))
+    relay_contexts(ctx_two, 1, 1, 0)
+    relay_contexts(ctx_two, 1, 1, 1)
+    average(0, keep_zero)
     collect(ctx_two, 1, 1)
     last_output(1)
     stats_one = send_stats(1)
-    average(0, keep_zero)
-    keep_one = scatter_rows(1, stats_one)
     final_zero, final_one = gather_of(0), gather_of(1)
     hopped(0)
     final_zero.begin()
     fin[0, member] = mean_in[0]
+    keep_one = scatter_rows(1, stats_one)
+    final_zero.middle()
     average(1, keep_one)
-    final_zero.middle()
     hopped(1)
     final_one.begin()
     fin[1, member] = mean_in[1]
@@ -813,14 +847,15 @@
     final_one.end()
     place_rows(1)
 
-    for wave in (wave_one, wave_two, wave_out):
+    for wave in waves + [wave_out]:
         wave.sent()
     final_zero.sent()
     final_one.sent()
     for tick, ctx in enumerate((ctx_one, ctx_two)):
         for which in range(3):
             for s in range(4):
-                ctx_copy(ctx, tick, s, which).wait_send()
+                for group in both:
+                    ctx_copy(ctx, tick, s, group, which).wait_send()
     for n in range(16):
         hop_copy(n).wait_send()
         pass_own(n, to_pair, 0).wait_send()
@@ -859,6 +894,7 @@
             pltpu.VMEM((2 * ROWS, 768), F32),
             pltpu.VMEM((2 * ROWS, 2048), BF16),
             pltpu.VMEM((2 * ROWS, 2048), BF16),
+            pltpu.VMEM((4, 2, SEQ, HEAD_WIDTH), BF16),
             pltpu.VMEM((2, 2 * ROWS, 16), BF16),
             pltpu.VMEM((2, SEQ), jnp.int32),
             pltpu.VMEM((2, 1, WIDTH), F32),
@@ -876,19 +912,19 @@
             pltpu.VMEM((2, 2, 16, 512), BF16),
             pltpu.VMEM((2, 2, 16, 512), BF16),
             pltpu.VMEM((2, MEMBERS, 2, 16, 512), BF16),
-            dma((3, 2)),
-            dma((3, 2, 7)),
+            dma((5, 2)),
+            dma((5, 2, 7)),
             dma((2, 2)),
             dma((2, 2, 15)),
             dma((9,)),
-            dma((2, 3, 4)),
-            dma((2, 3, 4)),
+            dma((2, 3, 8)),
+            dma((2, 3, 8)),
             dma((16,)),
             dma((16,)),
             dma((3, 16)),
             dma((3, 16)),
-            dma((23,)),
-            dma((23,)),
+            dma((24,)),
+            dma((24,)),
             dma((2,)),
             dma((2,)),
         ],
@@ -899,7 +935,9 @@
     )(
         hidden_input.reshape(2, SEQ, WIDTH),
         document_index[0],
-        query_key_value_weight[0].reshape(256, 1536),
+        jnp.concatenate(
+            [query_key_value_weight[0, :, :, 512:], query_key_value_weight[0, :, :, :512]], axis=-1
+        ).reshape(256, 1536),
         output_weight[0],
         adapter_down[0, 0].T,
         adapter_up[0, 0],

time: 157 us -> 174 us (1.11)
  Pallas kernels: 152 us -> 167 us
    pallas_call x1, Pallas kernels: 152 us -> 167 us  [per_device(): pl.pallas_call(kernel, out_shape=jax.ShapeDtypeStruct((ROWS, WIDTH // 2),...]
    squeeze x0 -> x2, local copies, waits for them, and re-layouts: none -> 2.54 us  [the longest x1 1.41 us: per_device(): query_key_value_weight[0, :, :, :512]]
where the time goes in v5:
time: 174 us
  Pallas kernels  167 us (96%)
  local copies, waits for them, and re-layouts  5.81 us (3%)
    pallas_call x1, Pallas kernels, per_device(): pl.pallas_call(kernel, out_shape=jax.ShapeDtypeStruct((ROWS, WIDTH // 2),...  167 us

profile of v5, /device:TPU:1, one launch (start us, length us, event | category | flops | bytes accessed | tf_op | source)
XLA Modules:
  0.0 173.8 jit_solution(8601195588698881093)
XLA Ops:
  0.0 1.1 slice_bitcast_fusion.1
  1.1 1.4 slice_bitcast_fusion
  2.5 0.7 pad_maximum_fusion
  3.2 1.0 copy.11
  4.2 167.2 %relay.1 = bf16[256,2048]{1,0:T(8,128)(2,1)} custom-call(bf16[2,128,4096]{2,1,0:T(8,128)(2,1)} %bitcast.18, s32[2,128]{1,0:T(2,128)} %bitcast.23, bf16[256,1536]{1,0:T(8,128)(2,1)} %bitcast.17, bf16[1024,256]{1,0:T(8,128)(2,1)} %bitcast.19, bf16[16,1024]{1,0:T(8,128)(2,1)} %bitcast.21, bf16[16,4096]{1,0:T(8,128)(2,1)} %bitcast.20, f32[1,4096]{1,0:T(1,128)} %bitcast.22, ...), custom_call_target="tpu_custom_call" | custom-call | tf_op jit(solution)/shard_map/relay/pallas_call | solution.py:884
  171.4 2.3 %copy.13 = bf16[1,2,128,2048]{3,2,1,0:T(8,128)(2,1)} copy(bf16[1,2,128,2048]{3,2,1,0:T(8,128)(2,1)} %bitcast.15) | data formatting | bytes 2097152

commit v6 on v4

--- a/solution.py
+++ b/solution.py
@@ -352,7 +352,6 @@
     share_h = misc(
         hidden_in.at[tensor], half_of(parity, tensor), 1, to_pair
     )
-    share_h.start()
     share_out = misc(
         out_in.at[:, pl.ds(pl.multiple_of(other * 128, 128), 128)],
         wo.at[index8, pl.ds(pl.multiple_of(tensor * 1024, 1024), 1024)],
@@ -365,8 +364,6 @@
         small.append(misc(down_in, down_all.at[parity, tensor], 5 + k, device))
         small.append(misc(final_in, final_all.at[parity, tensor], 8 + k, device))
     small.append(misc(docs_in, docs_next, 11, {"section": after}))
-    for copy in small:
-        copy.start()
     load_h.wait()
     loads[0].wait()
 
@@ -469,19 +466,22 @@
                 ).astype(BF16)
 
     wave_one.middle()
+    share_h.start()
+    for copy in small:
+        copy.start()
     seed_in = pltpu.make_async_remote_copy(
         rows_of(place.pair), rows_of(place.pair), misc_s.at[0], misc_r.at[0], to_pair, MESH
     )
     seed_in.wait_recv()
     wave_two.begin()
     wave_one.late()
+    wave_two.middle()
     pltpu.make_async_remote_copy(
         half_of(1 - parity, tensor), half_of(1 - parity, tensor), misc_s.at[1], misc_r.at[1],
         to_pair, MESH,
     ).wait_recv()
     pass_h = misc(half_of(1 - parity, tensor), half_of(1 - parity, tensor), 12, to_other)
     pass_h.start()
-    wave_two.middle()
     load_o.wait()
     share_in = wo.at[index8, pl.ds(pl.multiple_of(other * 1024, 1024), 1024)]
     pltpu.make_async_remote_copy(
@@ -616,6 +616,7 @@
     run(11, 16)
     for n in (9, 10, 11):
         relay(n)
+        arrive(n + 3)
 
     def complete(r):
         for n in range(16):
@@ -644,17 +645,14 @@
         return carry
 
     complete(0)
-    arrive(12)
     lax.fori_loop(0, 8, norm_second, 0)
-    arrive(13)
+    arrive(15)
     relay(12)
+    relay(13)
     project(0, 3)
-    arrive(14)
-    arrive(15)
-    relay(13)
-    attend(docs_next, ctx_two, 1, 0, 2)
     relay(14)
     relay(15)
+    attend(docs_next, ctx_two, 1, 0, 2)
     complete(1)
     lax.fori_loop(8, 16, norm_second, 0)
     project(3, 6)

time: 157 us -> 151 us (0.962)
  Pallas kernels: 152 us -> 146 us
    pallas_call x1, Pallas kernels: 152 us -> 146 us  [per_device(): pl.pallas_call(kernel, out_shape=jax.ShapeDtypeStruct((ROWS, WIDTH // 2),...]
where the time goes in v6:
time: 151 us
  Pallas kernels  146 us (97%)
  local copies, waits for them, and re-layouts  4.4 us (3%)
    pallas_call x1, Pallas kernels, per_device(): pl.pallas_call(kernel, out_shape=jax.ShapeDtypeStruct((ROWS, WIDTH // 2),...  146 us
    unnamed x2, local copies, waits for them, and re-layouts  4.4 us

profile of v6, /device:TPU:1, one launch (start us, length us, event | category | flops | bytes accessed | tf_op | source)
XLA Modules:
  0.0 150.9 jit_solution(1522031220266365133)
XLA Ops:
  0.0 2.1 %copy.11 = bf16[32,8,2,768]{3,1,2,0:T(8,128)(2,1)} copy(bf16[32,8,2,768]{3,2,1,0:T(2,128)(2,1)} %bitcast.15) | data formatting | bytes 1572864
  2.1 146.5 %relay.1 = bf16[256,2048]{1,0:T(8,128)(2,1)} custom-call(bf16[2,128,4096]{2,1,0:T(8,128)(2,1)} %bitcast.14, s32[2,128]{1,0:T(2,128)} %bitcast.20, bf16[256,1536]{1,0:T(8,128)(2,1)} %bitcast.13, bf16[1024,256]{1,0:T(8,128)(2,1)} %bitcast.16, bf16[16,1024]{1,0:T(8,128)(2,1)} %bitcast.18, bf16[16,4096]{1,0:T(8,128)(2,1)} %bitcast.17, f32[1,4096]{1,0:T(1,128)} %bitcast.19, ...), custom_call_target="tpu_custom_call" | custom-call | tf_op jit(solution)/shard_map/relay/pallas_call | solution.py:847
  148.6 2.3 %copy.13 = bf16[1,2,128,2048]{3,2,1,0:T(8,128)(2,1)} copy(bf16[1,2,128,2048]{3,2,1,0:T(8,128)(2,1)} %bitcast.12) | data formatting | bytes 2097152

commit v7 on v6

--- a/solution.py
+++ b/solution.py
@@ -596,10 +596,10 @@
     def run(lower, upper):
         for n in range(lower, upper):
             start_block(n)
-            if n >= 4:
-                arrive(n - 4)
-            if n >= 7:
-                relay(n - 7)
+            if n >= 3:
+                arrive(n - 3)
+            if n >= 5:
+                relay(n - 5)
 
     collect(ctx_one, 0, 0)
     wave_out.end(0)
@@ -614,9 +614,9 @@
     run(10, 11)
     wave_out.end(3)
     run(11, 16)
-    for n in (9, 10, 11):
-        relay(n)
-        arrive(n + 3)
+    relay(11)
+    arrive(13)
+    arrive(14)
 
     def complete(r):
         for n in range(16):

time: 151 us -> 150 us (level)
  no operation moved by 1% of the time
where the time goes in v7:
time: 150 us
  Pallas kernels  145 us (97%)
  local copies, waits for them, and re-layouts  4.4 us (3%)
    pallas_call x1, Pallas kernels, per_device(): pl.pallas_call(kernel, out_shape=jax.ShapeDtypeStruct((ROWS, WIDTH // 2),...  145 us
    unnamed x2, local copies, waits for them, and re-layouts  4.4 us

profile of v7, /device:TPU:1, one launch (start us, length us, event | category | flops | bytes accessed | tf_op | source)
XLA Modules:
  0.0 149.8 jit_solution(16367011294979838146)
XLA Ops:
  0.0 2.1 %copy.11 = bf16[32,8,2,768]{3,1,2,0:T(8,128)(2,1)} copy(bf16[32,8,2,768]{3,2,1,0:T(2,128)(2,1)} %bitcast.15) | data formatting | bytes 1572864
  2.1 145.4 %relay.1 = bf16[256,2048]{1,0:T(8,128)(2,1)} custom-call(bf16[2,128,4096]{2,1,0:T(8,128)(2,1)} %bitcast.14, s32[2,128]{1,0:T(2,128)} %bitcast.20, bf16[256,1536]{1,0:T(8,128)(2,1)} %bitcast.13, bf16[1024,256]{1,0:T(8,128)(2,1)} %bitcast.16, bf16[16,1024]{1,0:T(8,128)(2,1)} %bitcast.18, bf16[16,4096]{1,0:T(8,128)(2,1)} %bitcast.17, f32[1,4096]{1,0:T(1,128)} %bitcast.19, ...), custom_call_target="tpu_custom_call" | custom-call | tf_op jit(solution)/shard_map/relay/pallas_call | solution.py:847
  147.5 2.3 %copy.13 = bf16[1,2,128,2048]{3,2,1,0:T(8,128)(2,1)} copy(bf16[1,2,128,2048]{3,2,1,0:T(8,128)(2,1)} %bitcast.12) | data formatting | bytes 2097152

commit v8 on v7

--- a/solution.py
+++ b/solution.py
@@ -606,8 +606,9 @@
     run(0, 4)
     wave_out.cross_far()
     collect(ctx_one, 0, 1)
+    run(4, 6)
     wave_out.round_far()
-    run(4, 8)
+    run(6, 8)
     wave_out.end(1)
     run(8, 10)
     wave_out.end(2)

time: 150 us -> 148 us (0.987)
  Pallas kernels: 145 us -> 143 us
    pallas_call x1, Pallas kernels: 145 us -> 143 us  [per_device(): pl.pallas_call(kernel, out_shape=jax.ShapeDtypeStruct((ROWS, WIDTH // 2),...]
where the time goes in v8:
time: 148 us; the launch traced here: 147 us
  Pallas kernels  143 us (97%)
  local copies, waits for them, and re-layouts  4.4 us (3%)
    pallas_call x1, Pallas kernels, per_device(): pl.pallas_call(kernel, out_shape=jax.ShapeDtypeStruct((ROWS, WIDTH // 2),...  143 us
    unnamed x2, local copies, waits for them, and re-layouts  4.4 us

profile of v8, /device:TPU:1, one launch (start us, length us, event | category | flops | bytes accessed | tf_op | source)
XLA Modules:
  0.0 147.4 jit_solution(452635709304994022)
XLA Ops:
  0.0 2.1 %copy.11 = bf16[32,8,2,768]{3,1,2,0:T(8,128)(2,1)} copy(bf16[32,8,2,768]{3,2,1,0:T(2,128)(2,1)} %bitcast.15) | data formatting | bytes 1572864
  2.1 142.9 %relay.1 = bf16[256,2048]{1,0:T(8,128)(2,1)} custom-call(bf16[2,128,4096]{2,1,0:T(8,128)(2,1)} %bitcast.14, s32[2,128]{1,0:T(2,128)} %bitcast.20, bf16[256,1536]{1,0:T(8,128)(2,1)} %bitcast.13, bf16[1024,256]{1,0:T(8,128)(2,1)} %bitcast.16, bf16[16,1024]{1,0:T(8,128)(2,1)} %bitcast.18, bf16[16,4096]{1,0:T(8,128)(2,1)} %bitcast.17, f32[1,4096]{1,0:T(1,128)} %bitcast.19, ...), custom_call_target="tpu_custom_call" | custom-call | tf_op jit(solution)/shard_map/relay/pallas_call | solution.py:848
  145.1 2.3 %copy.13 = bf16[1,2,128,2048]{3,2,1,0:T(8,128)(2,1)} copy(bf16[1,2,128,2048]{3,2,1,0:T(8,128)(2,1)} %bitcast.12) | data formatting | bytes 2097152
